TPU v7x, 1024 devices: a whole 4x8x16 slice. The times are simulated.
1024 devices in a mesh: tm: 16 (over y, z_hi), rows: 8 (over z_lo), dp: 8 (over x, core).
Axes of the slice: x: 4, y: 8, z: 16 (z_hi: 2, z_lo: 8; z = z_hi * 8 + z_lo), core: 2. Of those that a mesh axis runs over, the one named last changes fastest.
Arguments:
- latent_grad: bfloat16 [589824, 64], P(('dp', 'tm'), 'rows'), parts along dimension 0, may hold values from -6 to 6
- features: bfloat16 [256, 96, 96, 384], P(('dp', 'tm'), 'rows'), parts along dimension 0, may hold values from -6 to 6
- head_weight: bfloat16 [432, 384], replicated, may hold values from -0.0625 to 0.0625
Outputs:
- grad_features: bfloat16 [256, 96, 96, 384], P(('dp', 'tm'), 'rows'), parts along dimension 0
- head_weight_grad: float32 [3456, 384], P('dp'), parts along dimension 0
There are 8 independent parts, one for each index of `dp`. A program takes and returns all parts, laid end to end along the dimension named above; an argument that names none is the same for every part. Nothing has to cross between parts.
All inputs are finite; a program needn't handle non-finite values.
Results may differ from a plain program's by a relative error of at most 0.0031.
Values may be sent and summed in bfloat16 or wider, within the bound.
A program may use at most 64 MiB of HBM per device.

v0:
```python
import math

import jax
import jax.numpy as jnp
from jax import lax
from jax.sharding import PartitionSpec as P


def shifted(value, axis, steps):
    count = lax.axis_size(axis)
    leading, last = (max(0, -steps), min(count, count - steps))
    return lax.ppermute(value, axis, [(source, source + steps) for source in range(leading, last)])


def extended_2(value, sides, width):
    for axis, dim in sides:
        size, length = (lax.axis_size(axis), value.shape[dim])
        up = [(i, (i + 1) % size) for i in range(size - 1)]
        down = [(j, i) for i, j in up]
        last = lax.slice_in_dim(value, length - width, length, axis=dim)
        leading = lax.slice_in_dim(value, 0, width, axis=dim)
        before = lax.ppermute(last, axis, up)
        after = lax.ppermute(leading, axis, down)
        value = jnp.concatenate([before, value, after], axis=dim)
    return value


def shards(latent_grad, features, head_weight):
    n_time = lax.axis_size("tm")
    n_rows = lax.axis_size("rows")
    frames, rows_here, width, channels = features.shape
    feat_dev = latent_grad.shape[1]
    latent_ch = feat_dev * n_rows // 4
    cycle = 2 * n_time
    per_band = rows_here // 2 * (width // 2) // cycle
    outgoing = latent_grad.reshape(n_time, frames, n_rows, per_band, 2, feat_dev)
    outgoing = outgoing.transpose(0, 2, 1, 3, 4, 5)
    moved = lax.all_to_all(
        outgoing.reshape(n_time * n_rows, -1),
        ("tm", "rows"),
        split_axis=0,
        concat_axis=0,
        tiled=True,
    )
    moved = moved.reshape(n_time, n_rows, frames, per_band, 2, feat_dev)
    first = moved[:, :, :, :, 0, :]
    second = moved[::-1, :, :, :, 1, :]
    ordered = jnp.concatenate([first, second], axis=0)
    ordered = ordered.transpose(2, 3, 0, 1, 4)
    grid = ordered.reshape(frames, rows_here // 2, width // 2, latent_ch, 2, 2)
    grid = grid.transpose(0, 1, 4, 2, 5, 3).reshape(frames, rows_here, width, latent_ch)
    later = shifted(grid, "tm", -1)
    extended = jnp.concatenate([grid, later], axis=0)
    extended = extended_2(extended, (("rows", 1),), 1)
    extended = jnp.pad(extended, ((0, 0), (0, 0), (1, 1), (0, 0)))
    pieces = []
    for kt in range(3):
        for kh in range(3):
            for kw in range(3):
                pieces.append(
                    extended[
                        2 - kt : 2 - kt + frames,
                        2 - kh : 2 - kh + rows_here,
                        2 - kw : 2 - kw + width,
                        :,
                    ]
                )
    cols = jnp.concatenate(pieces, axis=-1).reshape(frames * rows_here * width, 27 * latent_ch)
    hidden = features.reshape(-1, channels).astype(jnp.float32)
    sig = jax.nn.sigmoid(hidden)
    act = (hidden * sig).astype(jnp.bfloat16)
    scale = 1.0 / math.sqrt(frames * n_time * rows_here * n_rows * width)
    partial_grad = (
        lax.dot_general(cols, act, (((0,), (0,)), ((), ())), preferred_element_type=jnp.float32)
        * scale
    )
    weight_grad = lax.psum(partial_grad, ("tm", "rows"))
    pre = jnp.dot(cols, head_weight, preferred_element_type=jnp.float32)
    grad_features = (pre * sig * (1.0 + hidden * (1.0 - sig))).astype(jnp.bfloat16)
    return (grad_features.reshape(features.shape), weight_grad)


def solution(mesh):
    return jax.shard_map(
        shards,
        mesh=mesh,
        in_specs=(P(("dp", "tm"), "rows"), P(("dp", "tm"), "rows", None, None), P()),
        out_specs=(P(("dp", "tm"), "rows", None, None), P("dp", None)),
        check_vma=False,
    )
```

profile of v0, /device:TPU:6, one launch (start us, length us, event | category | flops | bytes accessed | tf_op | source)
XLA Modules:
  0.0 394.8 jit_solution(5405301792176985372)
XLA Ops:
  7.2 1.4 copy.67
  8.7 0.8 copy.81
  9.5 1.4 reshape.64
  10.9 0.5 broadcast.36
  11.4 1.3 reduce
  12.8 44.8 %all_to_all.9 = bf16[128,2,144]{2,1,0:T(2,128)(2,1)S(1)} all-to-all(bf16[128,2,144]{2,1,0:T(2,128)(2,1)S(1)} %reshape.65), channel_id=1, replica_groups=mesh['tm'=16,'rows'=8,'dp'=8] {'tm','rows'}, dimensions={0} | all-to-all | bytes 147456 | tf_op jit(solution)/shard_map/all_to_all | solution.py:38
  57.9 1.3 reshape.58
  59.6 0.5 rev.3
  62.2 1.3 collective-permute-start
  63.5 13.9 %collective-permute-done = bf16[2,12,96,16]{2,3,1,0:T(8,128)(2,1)S(1)} collective-permute-done((bf16[2,12,96,16]{2,3,1,0:T(8,128)(2,1)S(1)}, bf16[2,12,96,16]{2,3,1,0:T(8,128)(2,1)S(1)}, u32[]{:S(2)}, u32[]{:S(2)}) %collective-permute-start) | collective-permute-done | bytes 73760 | tf_op jit(solution)/shard_map/ppermute | solution.py:12
  77.8 7.5 %collective-permute-start.1 = (bf16[4,1,96,16]{3,2,1,0:T(8,128)(2,1)S(1)}, bf16[4,1,96,16]{3,2,1,0:T(8,128)(2,1)S(1)}, u32[]{:S(2)}, u32[]{:S(2)}) collective-permute-start(bf16[4,1,96,16]{3,2,1,0:T(8,128)(2,1)S(1)} %get-tuple-element.30), channel_id=1, source_target_pairs={{0,8},{8,16},{16,24},{24,32},{32,40},{40,48},{48,56},{1,9},{9,17},... | collective-permute-start | bytes 36872 | tf_op jit(solution)/shard_map/ppermute | solution.py:22
  85.2 1.5 collective-permute-start.2
  86.7 1.0 pad_maximum_fusion.1
  87.7 4.1 %collective-permute-done.2 = bf16[4,1,96,16]{3,2,1,0:T(8,128)(2,1)S(1)} collective-permute-done((bf16[4,1,96,16]{3,2,1,0:T(8,128)(2,1)S(1)}, bf16[4,1,96,16]{3,2,1,0:T(8,128)(2,1)S(1)}, u32[]{:S(2)}, u32[]{:S(2)}) %collective-permute-start.2) | collective-permute-done | bytes 12320 | tf_op jit(solution)/shard_map/ppermute | solution.py:23
  91.8 0.6 select_maximum_fusion
  92.3 4.4 %fusion.23 = (bf16[2,12,96,16]{3,2,1,0:T(8,128)(2,1)}, bf16[2,12,96,16]{3,2,1,0:T(8,128)(2,1)}, bf16[2,12,96,16]{3,2,1,0:T(8,128)(2,1)}, bf16[2,12,96,16]{3,2,1,...) fusion(bf16[4,14,98,16]{3,2,1,0:T(8,128)(2,1)S(1)} %select_maxi, ...), kind=kLoop, calls=%fused_computation.34 | loop fusion | bytes 2654208 | tf_op jit(solution)/shard_map/slice | solution.py:61
  97.0 1.5 fusion.24
  98.5 14.1 %concatenate.112 = bf16[2,12,96,432]{3,2,1,0:T(8,128)(2,1)} concatenate(bf16[2,12,96,16]{3,2,1,0:T(8,128)(2,1)} %get-tuple-element.21, bf16[2,12,96,16]{3,2,1,0:T(8,128)(2,1)} %get-tuple-element.34, bf16[2,12,96,16]{3,2,1,0:T(8,128)(2,1)} %get-tuple-element.20, bf16[2,12,96,16]{3,2,1,0:T(8,128)(2,1)} %get-tuple-element.19, bf16[2,12,96,16]{3,2,1,0:T(8,128)(2,1)S(1)} %copy.76, ...), dimensions={3} | concatenate | bytes 3981312 | tf_op jit(solution)/shard_map/concatenate | solution.py:68
  112.6 4.3 %fusion.19 = f32[432,384]{1,0:T(8,128)} fusion(bf16[2,12,96,432]{3,2,1,0:T(8,128)(2,1)} %concatenate.112, bf16[2,12,96,384]{3,2,1,0:T(8,128)(2,1)} %param.4), kind=kOutput, calls=%fused_computation.27 | convolution fusion | flops 769886208 | bytes 4423680 | tf_op jit(solution)/shard_map/dot_general | solution.py:74
  117.0 5.3 %fusion.8 = (f32[2304,384]{1,0:T(8,128)}, f32[2304,384]{1,0:T(8,128)}) fusion(bf16[2,12,96,384]{3,2,1,0:T(8,128)(2,1)} %param.4), kind=kLoop, calls=%fused_computation.15 | loop fusion | flops 6193152 | bytes 8847360 | tf_op jit(solution)/shard_map/div | solution.py:70
  122.3 14.2 %concatenate.111 = bf16[2304,432]{1,0:T(8,128)(2,1)} concatenate(bf16[2304,16]{1,0:T(8,128)(2,1)} %bitcast.96, bf16[2304,16]{1,0:T(8,128)(2,1)} %bitcast.75, bf16[2304,16]{1,0:T(8,128)(2,1)} %bitcast.95, bf16[2304,16]{1,0:T(8,128)(2,1)} %bitcast.94, bf16[2304,16]{1,0:T(8,128)(2,1)S(1)} %bitcast.71, bf16[2304,16]{1,0:T(8,128)(2,1)} %bitcast.93, bf16[2304,16]{1,0:T(8,128)(2,1)} %bitcast.92, ...), dimensions={1} | concatenate | bytes 3981312 | tf_op jit(solution)/shard_map/concatenate | solution.py:68
  136.5 6.4 %fusion.1 = bf16[2304,384]{1,0:T(8,128)(2,1)} fusion(f32[2304,384]{1,0:T(8,128)} %get-tuple-element.3, f32[2304,384]{1,0:T(8,128)} %get-tuple-element.2, bf16[2304,432]{1,0:T(8,128)(2,1)} %concatenate.111, bf16[432,384]{1,0:T(8,128)(2,1)S(1)} %copy-done), kind=kOutput, calls=%fused_computation.4 | convolution fusion | flops 767066112 | bytes 11169792 | tf_op jit(solution)/shard_map/dot_general | solution.py:78
  142.9 243.1 %all-reduce.3.cloned.1.call-done = f32[432,384]{1,0:T(8,128)} async-done(((f32[432,384]{1,0:T(8,128)}), f32[432,384]{1,0:T(8,128)}) %all-reduce.3.cloned.1.call-update) | async-done | bytes 663568 | tf_op jit(solution)/shard_map/psum | solution.py:77
  386.0 2.0 copy.84
  (19 shorter events, 3.5 us)
Async XLA Ops:
  7.2 129.3 %copy-start = (bf16[432,384]{1,0:T(8,128)(2,1)S(1)}, bf16[432,384]{1,0:T(8,128)(2,1)}, u32[]{:S(2)}) copy-start(bf16[432,384]{1,0:T(8,128)(2,1)} %param.5) | copy-start | bytes 995332
  7.2 378.8 %all-reduce.3.cloned.1.call-start = ((), (), s32[]{:S(2)}) async-start(), calls=%async_computation.1 | async-start | bytes 1327104 | tf_op jit(solution)/shard_map/psum | solution.py:77
  62.2 15.2 %collective-permute-start = (bf16[2,12,96,16]{2,3,1,0:T(8,128)(2,1)S(1)}, bf16[2,12,96,16]{2,3,1,0:T(8,128)(2,1)S(1)}, u32[]{:S(2)}, u32[]{:S(2)}) collective-permute-start(bf16[2,12,96,16]{2,3,1,0:T(8,128)(2,1)S(1)} %copy.75), channel_id=1, source_target_pairs={{64,0},{128,64},{192,128},{256,192},{320,256},{384,320},{448,384},... | collective-permute-start | bytes 221192 | tf_op jit(solution)/shard_map/ppermute | solution.py:12
  77.8 9.9 %collective-permute-start.1 = (bf16[4,1,96,16]{3,2,1,0:T(8,128)(2,1)S(1)}, bf16[4,1,96,16]{3,2,1,0:T(8,128)(2,1)S(1)}, u32[]{:S(2)}, u32[]{:S(2)}) collective-permute-start(bf16[4,1,96,16]{3,2,1,0:T(8,128)(2,1)S(1)} %get-tuple-element.30), channel_id=1, source_target_pairs={{0,8},{8,16},{16,24},{24,32},{32,40},{40,48},{48,56},{1,9},{9,17},... | collective-permute-start | bytes 36872 | tf_op jit(solution)/shard_map/ppermute | solution.py:22
  85.2 6.5 %collective-permute-start.2 = (bf16[4,1,96,16]{3,2,1,0:T(8,128)(2,1)S(1)}, bf16[4,1,96,16]{3,2,1,0:T(8,128)(2,1)S(1)}, u32[]{:S(2)}, u32[]{:S(2)}) collective-permute-start(bf16[4,1,96,16]{3,2,1,0:T(8,128)(2,1)S(1)} %get-tuple-element.31), channel_id=1, source_target_pairs={{8,0},{16,8},{24,16},{32,24},{40,32},{48,40},{56,48},{9,1},{17,9},... | collective-permute-start | bytes 36872 | tf_op jit(solution)/shard_map/ppermute | solution.py:23
Sparse Core Ops, SparseCore 0:
  117.1 268.8 all-reduce.2
where the time goes:
time: 399 us; the launch traced here: 395 us
  waiting for transfers between devices  261 us (65%)
  local copies, waits for them, and re-layouts  45.1 us (11%)
  blocking collectives  44.8 us (11%)
  between operations  14.2 us (4%)
  matrix products  10.7 us (3%)
  starting transfers between devices  10.3 us (3%)
  other arithmetic  8.62 us (2%)
    psum x1, waiting for transfers between devices, shards(): weight_grad = lax.psum(partial_grad, ('tm', 'rows'))  243 us
    all_to_all x1, blocking collectives, shards(): lax.all_to_all(outgoing.reshape(n_time * n_rows, -1), ('tm', 'rows'), spl...  44.8 us
    concatenate x2, local copies, waits for them, and re-layouts, shards(): jnp.concatenate(pieces, axis=-1)  28.3 us
    ppermute x1, waiting for transfers between devices, shifted(): lax.ppermute(value, axis, [(source, source + steps) for source in range(l...  13.9 us
  transfers between devices with their start and end apart: 4, of which 3 were waited for; matrix products, arithmetic and copies ran while one was open for 7% of the time, Pallas kernels for 0%

commit v1 on v0

v1 whole, which is shorter than its diff:
```python
import math

import jax
import jax.numpy as jnp
from jax import lax
from jax.experimental import pallas as pl
from jax.experimental.pallas import tpu as pltpu
from jax.sharding import PartitionSpec as P

NY = 8
NZ = 16
OWN = 11
MESH = pl.DeviceIdType.MESH
Y_ORDER = (4, 3, 5, 2, 6, 1, 7)
Z_ORDER = (8, 7, 9, 6, 10, 5, 11, 4, 12, 3, 13, 2, 14, 1, 15)


def kernel(scale, lat, feat, weight, grad_out, sum_out, xf, act, dsl, gout, lp, send, rx1, rx2, perm, ts, os_, gt, cols, sb, rb, sb2, rb2, az, ay, in_sem, out_sem, loc_sem, sa, ra, sz, rz, sc, rc, sd, rd, se, re, sf, rf):
    tm = lax.axis_index("tm")
    rows = lax.axis_index("rows")
    y = lax.div(tm, 2)
    zh = lax.rem(tm, 2)
    z = zh * 8 + rows

    def y_dev(d):
        other = lax.rem(y + d, NY)
        return other, {"tm": other * 2 + zh}

    def z_dev(d):
        other = lax.rem(z + d, NZ)
        return other, {"tm": y * 2 + lax.div(other, 8), "rows": lax.rem(other, 8)}

    load = pltpu.make_async_copy(feat, xf, in_sem)
    load.start()

    barrier = pltpu.get_barrier_semaphore()
    for d in range(1, NY):
        pl.semaphore_signal(barrier, inc=1, device_id=y_dev(d)[1], device_id_type=MESH)
    for d in range(1, NZ):
        pl.semaphore_signal(barrier, inc=1, device_id=z_dev(d)[1], device_id_type=MESH)

    lp[:, 0:128] = jnp.zeros((8, 128), jnp.float32)
    lp[:, 128:4736] = lat[...].astype(jnp.float32)
    lp[:, 4736:5248] = jnp.zeros((8, 512), jnp.float32)
    lane8 = lax.broadcasted_iota(jnp.int32, (8, 128), 1)

    def pack(pair, carry):
        base = pl.multiple_of(pair * 1152, 128)
        for y2 in range(2):
            for zd in range(16):
                value = jnp.zeros((8, 128), jnp.float32)
                for tt in range(4):
                    start = 128 + 576 * y2 + 288 * (zd // 8) + 144 * tt + 18 * (zd % 8) - 6
                    v, l = start // 128, start % 128
                    shift = (32 * tt - l) % 128
                    piece = lp[:, pl.ds(base + 128 * v, 128)]
                    piece = pltpu.roll(piece, shift, 1) if shift else piece
                    if l > 96:
                        nxt = lp[:, pl.ds(base + 128 * v + 128, 128)]
                        nxt = pltpu.roll(nxt, shift, 1) if shift else nxt
                        piece = jnp.where(lane8 < 32 * tt + 128 - l, piece, nxt)
                    value = piece if tt == 0 else jnp.where(lane8 < 32 * tt, value, piece)
                send[pair * 2 + y2, zd] = value.astype(jnp.bfloat16)
        return carry

    lax.fori_loop(0, 4, pack, 0)
    pl.semaphore_wait(barrier, NY + NZ - 2)

    first = []
    for d in Y_ORDER:
        other, dev = y_dev(d)
        copy = pltpu.make_async_remote_copy(send.at[other], rx1.at[y], sa.at[d], ra.at[d], device_id=dev, device_id_type=MESH)
        copy.start()
        first.append(copy)
    own1 = pltpu.make_async_copy(send.at[y], rx1.at[y], loc_sem.at[0])
    own1.start()

    row = lax.broadcasted_iota(jnp.int32, (256, 256), 0)
    col = lax.broadcasted_iota(jnp.int32, (256, 256), 1)
    source = ((row >> 3) & 7) * 2 + ((row >> 6) & 1)
    token = jnp.where(row < 128, source, 31 - source)
    target = ((row >> 2) & 1) * 128 + ((row >> 1) & 1) * 64 + token * 2 + (row & 1)
    perm[...] = jnp.where(col == target, 1.0, 0.0).astype(jnp.bfloat16)

    load.wait()

    def silu(step, carry):
        at = pl.ds(pl.multiple_of(step * 64, 64), 64)
        x = xf[at, :].astype(jnp.float32)
        sig = 1.0 / (1.0 + jnp.exp(-x))
        act[at, :] = (x * sig).astype(jnp.bfloat16)
        dsl[at, :] = sig * (1.0 + x * (1.0 - sig))
        return carry

    lax.fori_loop(0, 36, silu, 0)

    own1.wait()
    for copy in first:
        copy.wait()

    second = []
    for d in Z_ORDER:
        other, dev = z_dev(d)
        copy = pltpu.make_async_remote_copy(rx1.at[:, other], rx2.at[z], sz.at[d], rz.at[d], device_id=dev, device_id_type=MESH)
        copy.start()
        second.append(copy)
    own2 = pltpu.make_async_copy(rx1.at[:, z], rx2.at[z], loc_sem.at[1])
    own2.start()
    own2.wait()
    for copy in second:
        copy.wait()

    for r in range(8):
        low = rx2[r].astype(jnp.float32).reshape(64, 128)
        high = rx2[8 + r].astype(jnp.float32).reshape(64, 128)
        ts[r] = jnp.concatenate([low, high], axis=0).T
    for r in range(8):
        even = ts[r, pl.ds(0, 64, stride=2), :]
        odd = ts[r, pl.ds(1, 64, stride=2), :]
        left = jnp.concatenate([even, odd], axis=1).astype(jnp.bfloat16)
        moved = jnp.dot(left, perm[...], preferred_element_type=jnp.float32)
        os_[0, r * 64:(r + 1) * 64, :] = moved[:, 0:128]
        os_[1, r * 64:(r + 1) * 64, :] = moved[:, 128:256]
    top = rows == 0
    bottom = rows == 7
    for t in range(4):
        for g in range(5):
            for e in range(2):
                k0, k1, k2 = [os_[e, pl.ds(t * 16 + 3 * g + k, 8, stride=64), :] for k in range(3)]
                at = pl.ds(t * 16 + e, 8, stride=2)
                k1_64 = pltpu.roll(k1, 64, 1)
                k2_96 = pltpu.roll(k2, 96, 1)
                k0_32 = pltpu.roll(k0, 32, 1)
                if g > 0:
                    v0 = jnp.where(lane8 < 64, k0, jnp.where(lane8 < 96, k1_64, k0_32))
                    if g == 4:
                        v0 = jnp.where(bottom, 0.0, v0)
                    gt[3 * g, at, :] = v0
                if 0 < g < 4:
                    v1 = jnp.where(lane8 < 64, jnp.where(lane8 < 32, k0_32, pltpu.roll(k1, 96, 1)), jnp.where(lane8 < 96, pltpu.roll(k1, 32, 1), k2_96))
                    gt[3 * g + 1, at, :] = v1
                if g < 4:
                    v2 = jnp.where(lane8 < 32, k2_96, jnp.where(lane8 < 64, k1_64, k2))
                    if g == 0:
                        v2 = jnp.where(top, 0.0, v2)
                    gt[3 * g + 2, at, :] = v2

    place = lax.rem(lax.broadcasted_iota(jnp.int32, (16, 1152), 1), 96)
    for t in range(4):
        grid = jnp.concatenate([gt[v, 16 * t:16 * t + 16, :] for v in range(2, 13)], axis=1)
        for kh in range(3):
            for kw in range(3):
                off = 128 + (1 - kh) * 96 + 1 - kw
                block = (pltpu.roll(grid, 1408 - off, 1) if off % 1408 else grid)[:, 0:1152]
                if kw == 0:
                    block = jnp.where(place == 95, 0.0, block)
                if kw == 2:
                    block = jnp.where(place == 0, 0.0, block)
                at = (3 - t) * 144 + (kh * 3 + kw) * 16
                cols[at:at + 16, :] = block.astype(jnp.bfloat16)

    for c in range(3):
        lanes = slice(128 * c, 128 * c + 128)
        total = jnp.dot(cols[144:576, :], act[0:1152, lanes], preferred_element_type=jnp.float32)
        total = total + jnp.dot(cols[0:432, :], act[1152:2304, lanes], preferred_element_type=jnp.float32)
        sb[27 * c:27 * c + 27] = total.reshape(27, 16, 128).astype(jnp.bfloat16)
    sb[81:88] = jnp.zeros((7, 16, 128), jnp.bfloat16)

    third = []
    for d in Y_ORDER:
        other, dev = y_dev(d)
        copy = pltpu.make_async_remote_copy(sb.at[pl.ds(other * OWN, OWN)], rb.at[d], sc.at[d], rc.at[d], device_id=dev, device_id_type=MESH)
        copy.start()
        third.append(copy)

    for t in range(2):
        def backward(step, carry):
            lanes = pl.ds(pl.multiple_of(step * 384, 128), 384)
            at = pl.ds(pl.multiple_of(t * 1152 + step * 384, 128), 384)
            pre = lax.dot_general(cols[(1 - t) * 144:(1 - t) * 144 + 432, lanes], weight[...], (((0,), (0,)), ((), ())), preferred_element_type=jnp.float32)
            gout[at, :] = (pre * dsl[at, :]).astype(jnp.bfloat16)
            return carry

        lax.fori_loop(0, 3, backward, 0)
    store = pltpu.make_async_copy(gout, grad_out, out_sem)
    store.start()

    for copy in third:
        copy.wait()
    part = sb[pl.ds(y * OWN, OWN)].astype(jnp.float32)
    for d in range(1, NY):
        part = part + rb[d].astype(jnp.float32)
    sb2[...] = part.astype(jnp.bfloat16)

    for d in Z_ORDER:
        other, dev = z_dev(d)

        @pl.when(other < OWN)
        def _():
            pltpu.make_async_remote_copy(sb2.at[other], rb2.at[d], sd.at[d], rd.at[d], device_id=dev, device_id_type=MESH).start()

    @pl.when(z < OWN)
    def _():
        for d in range(1, NZ):
            pltpu.make_async_remote_copy(sb2.at[0], rb2.at[d], sd.at[d], rd.at[d], device_id=z_dev(d)[1], device_id_type=MESH).wait_recv()
        whole = sb2[z].astype(jnp.float32)
        for d in range(1, NZ):
            whole = whole + rb2[d].astype(jnp.float32)
        az[z] = (whole * scale).astype(jnp.bfloat16)
        for d in Z_ORDER:
            pltpu.make_async_remote_copy(az.at[z], az.at[z], se.at[d], re.at[d], device_id=z_dev(d)[1], device_id_type=MESH).start()

    for d in range(1, NZ):
        @pl.when(lax.rem(z + NZ - d, NZ) < OWN)
        def _():
            pltpu.make_async_remote_copy(az.at[0], az.at[0], se.at[d], re.at[d], device_id=z_dev(d)[1], device_id_type=MESH).wait_recv()

    last = []
    for d in Y_ORDER:
        other, dev = y_dev(d)
        copy = pltpu.make_async_remote_copy(az, ay.at[y], sf.at[d], rf.at[d], device_id=dev, device_id_type=MESH)
        copy.start()
        last.append(copy)
    sum_out[pl.ds(y * OWN, OWN)] = az[...]
    for d in range(1, NZ):
        @pl.when(lax.rem(z + d, NZ) < OWN)
        def _():
            pltpu.make_async_remote_copy(sb2.at[0], rb2.at[d], sd.at[d], rd.at[d], device_id=z_dev(d)[1], device_id_type=MESH).wait_send()

    @pl.when(z < OWN)
    def _():
        for d in range(1, NZ):
            pltpu.make_async_remote_copy(az.at[0], az.at[0], se.at[d], re.at[d], device_id=z_dev(d)[1], device_id_type=MESH).wait_send()

    for copy in last:
        copy.wait()
    for d in range(1, NY):
        other = lax.rem(y + NY - d, NY)
        sum_out[pl.ds(other * OWN, OWN)] = ay[other]
    store.wait()


def shards(latent_grad, features, head_weight):
    frames, rows_here, width, channels = features.shape
    cells = frames * rows_here * width
    scale = 1.0 / math.sqrt(cells * NY * NZ)
    bf, f32 = jnp.bfloat16, jnp.float32
    dma = pltpu.SemaphoreType.DMA
    vmem = pl.BlockSpec(memory_space=pltpu.VMEM)
    hbm = pl.BlockSpec(memory_space=pl.ANY)
    grad, total = pl.pallas_call(
        lambda *refs: kernel(scale, *refs),
        out_shape=(
            jax.ShapeDtypeStruct((cells, channels), bf),
            jax.ShapeDtypeStruct((NY * OWN, 16, 128), bf),
        ),
        in_specs=[vmem, hbm, vmem],
        out_specs=(hbm, vmem),
        scratch_shapes=[
            pltpu.VMEM((cells, channels), bf),
            pltpu.VMEM((cells, channels), bf),
            pltpu.VMEM((cells, channels), f32),
            pltpu.VMEM((cells, channels), bf),
            pltpu.VMEM((8, 5248), f32),
            pltpu.VMEM((NY, NZ, 8, 128), bf),
            pltpu.VMEM((NY, NZ, 8, 128), bf),
            pltpu.VMEM((NZ, NY, 8, 128), bf),
            pltpu.VMEM((256, 256), bf),
            pltpu.VMEM((8, 128, 128), f32),
            pltpu.VMEM((2, 512, 128), f32),
            pltpu.VMEM((15, 64, 128), f32),
            pltpu.VMEM((576, 1152), bf),
            pltpu.VMEM((NY * OWN, 16, 128), bf),
            pltpu.VMEM((NY, OWN, 16, 128), bf),
            pltpu.VMEM((OWN, 16, 128), bf),
            pltpu.VMEM((NZ, 16, 128), bf),
            pltpu.VMEM((OWN, 16, 128), bf),
            pltpu.VMEM((NY, OWN, 16, 128), bf),
            dma, dma, dma((2,)),
            dma((NY,)), dma((NY,)), dma((NZ,)), dma((NZ,)),
            dma((NY,)), dma((NY,)), dma((NZ,)), dma((NZ,)),
            dma((NZ,)), dma((NZ,)), dma((NY,)), dma((NY,)),
        ],
        compiler_params=pltpu.CompilerParams(collective_id=0, has_side_effects=True),
        name="encoder_head_backward",
    )(latent_grad.T, features.reshape(cells, channels), head_weight)
    total = total[:81].reshape(3, 432, 128).transpose(1, 0, 2).reshape(432, 384)
    return grad.reshape(features.shape), total.astype(f32)


def solution(mesh):
    return jax.shard_map(
        shards,
        mesh=mesh,
        in_specs=(P(("dp", "tm"), "rows"), P(("dp", "tm"), "rows", None, None), P()),
        out_specs=(P(("dp", "tm"), "rows", None, None), P("dp", None)),
        check_vma=False,
    )
```

time: 399 us -> 84.7 us (0.21)
  waiting for transfers between devices: 261 us -> 0 us
  Pallas kernels: 0 us -> 80.1 us
  blocking collectives: 44.8 us -> 0 us
  local copies, waits for them, and re-layouts: 45.1 us -> 3.61 us
  between operations: 14.2 us -> 0.67 us
  matrix products: 10.7 us -> 0 us
  starting transfers between devices: 10.3 us -> 0 us
  other arithmetic: 8.62 us -> 0.05 us
    psum x1 -> x0, waiting for transfers between devices: 243 us -> none  [shards(): weight_grad = lax.psum(partial_grad, ('tm', 'rows'))]
    pallas_call x0 -> x1, Pallas kernels: none -> 80.1 us  [shards(): pl.pallas_call(lambda *refs: kernel(scale, *refs), out_shape=(jax.ShapeDt...]
    all_to_all x1 -> x0, blocking collectives: 44.8 us -> none  [shards(): lax.all_to_all(outgoing.reshape(n_time * n_rows, -1), ('tm', 'rows'), spl...]
    concatenate x2 -> x0, local copies, waits for them, and re-layouts: 28.3 us -> none  [shards(): jnp.concatenate(pieces, axis=-1)]
    ppermute x3 -> x0, waiting for transfers between devices: 18 us -> none  [the longest x1 13.9 us: shifted(): lax.ppermute(value, axis, [(source, source + steps) for source in range(l...]
    dot_general x2 -> x0, matrix products: 10.7 us -> none  [the longest x1 6.37 us: shards(): pre = jnp.dot(cols, head_weight, preferred_element_type=jnp.float32)]
    ppermute x3 -> x0, starting transfers between devices: 10.2 us -> none  [the longest x1 7.47 us: extended_2(): before = lax.ppermute(last, axis, up)]
    div x1 -> x0, other arithmetic: 5.31 us -> none  [shards(): sig = jax.nn.sigmoid(hidden)]
  transfers between devices with their start and end apart: 4 -> 0, of which waited for: 3 -> 0; matrix products, arithmetic and copies ran while one was open for 7% -> 0% of each run, Pallas kernels for 0% -> 0%
where the time goes in v1:
time: 84.7 us; the launch traced here: 84.4 us
  Pallas kernels  80.1 us (95%)
  local copies, waits for them, and re-layouts  3.61 us (4%)
    pallas_call x1, Pallas kernels, shards(): pl.pallas_call(lambda *refs: kernel(scale, *refs), out_shape=(jax.ShapeDt...  80.1 us
    unnamed x4, local copies, waits for them, and re-layouts  2.35 us

profile of v1, /device:TPU:6, one launch (start us, length us, event | category | flops | bytes accessed | tf_op | source)
XLA Modules:
  0.0 84.4 jit_solution(1067596205442947002)
XLA Ops:
  0.6 80.1 %encoder_head_backward.1 = (bf16[2304,384]{1,0:T(8,128)(2,1)}, bf16[88,16,128]{2,1,0:T(8,128)(2,1)}) custom-call(bf16[8,4608]{1,0:T(8,128)(2,1)} %bitcast.14, bf16[2304,384]{1,0:T(8,128)(2,1)} %bitcast.12, bf16[432,384]{1,0:T(8,128)(2,1)} %refs_2_.1), custom_call_target="tpu_custom_call" | custom-call | tf_op jit(solution)/shard_map/encoder_head_backward/pallas_call | solution.py:251
  80.8 1.0 %slice.3 = bf16[81,16,128]{2,1,0:T(8,128)(2,1)S(1)} slice(bf16[88,16,128]{2,1,0:T(8,128)(2,1)} %get-tuple-element.5), slice={[0:81], [0:16], [0:128]} | slice | bytes 663552 | tf_op jit(solution)/shard_map/slice | solution.py:287
  81.8 0.0 copy-start
  81.8 0.3 copy.6
  82.1 1.1 %copy.7 = f32[432,384]{1,0:T(8,128)} copy(f32[432,384]{0,1:T(8,128)S(1)} %bitcast.10) | data formatting | bytes 1327104
  83.2 0.1 copy-done
  83.2 1.2 %copy.9 = bf16[2,12,96,384]{3,2,1,0:T(8,128)(2,1)} copy(bf16[2,12,96,384]{3,2,1,0:T(8,128)(2,1)S(1)} %bitcast.11) | data formatting | bytes 3538944
  (1 shorter events, 0.0 us)
Async XLA Ops:
  81.8 1.5 %copy-start = (bf16[2304,384]{1,0:T(8,128)(2,1)S(1)}, bf16[2304,384]{1,0:T(8,128)(2,1)}, u32[]{:S(2)}) copy-start(bf16[2304,384]{1,0:T(8,128)(2,1)} %get-tuple-element.4) | copy-start | bytes 5308420

commit v2 on v1

--- a/solution.py
+++ b/solution.py
@@ -9,13 +9,18 @@
 
 NY = 8
 NZ = 16
-OWN = 11
+OWN_A = 14
+OWN_B = 4
+ALL_A = 112
+USED_A = 98
 MESH = pl.DeviceIdType.MESH
 Y_ORDER = (4, 3, 5, 2, 6, 1, 7)
+SLOTS = (0, 1, 7, 2, 6, 3, 5, 4)
+GROUPS = ((0, 1), (1, 3), (3, 5), (5, 8))
 Z_ORDER = (8, 7, 9, 6, 10, 5, 11, 4, 12, 3, 13, 2, 14, 1, 15)
 
 
-def kernel(scale, lat, feat, weight, grad_out, sum_out, xf, act, dsl, gout, lp, send, rx1, rx2, perm, ts, os_, gt, cols, sb, rb, sb2, rb2, az, ay, in_sem, out_sem, loc_sem, sa, ra, sz, rz, sc, rc, sd, rd, se, re, sf, rf):
+def kernel(scale, lat_hbm, feat, weight_hbm, grad_out, sum_out, lat, weight, xf, act, dsl, gout, lp, send, rx1, rx2, perm, ts, os_, gt, cols, sa, sb, ra, rb, pa, qa, pb, qb, fin, in_sem, out_sem, sy, ry, sz, rz, s1a, r1a, s1b, r1b, s2a, r2a, s2b, r2b, s3a, r3a, s3b, r3b, s4a, r4a, s4b, r4b):
     tm = lax.axis_index("tm")
     rows = lax.axis_index("rows")
     y = lax.div(tm, 2)
@@ -30,8 +35,12 @@
         other = lax.rem(z + d, NZ)
         return other, {"tm": y * 2 + lax.div(other, 8), "rows": lax.rem(other, 8)}
 
-    load = pltpu.make_async_copy(feat, xf, in_sem)
+    load_lat = pltpu.make_async_copy(lat_hbm, lat, in_sem.at[0])
+    load_lat.start()
+    load = pltpu.make_async_copy(feat, xf, in_sem.at[1])
     load.start()
+    load_weight = pltpu.make_async_copy(weight_hbm, weight, in_sem.at[2])
+    load_weight.start()
 
     barrier = pltpu.get_barrier_semaphore()
     for d in range(1, NY):
@@ -40,6 +49,7 @@
         pl.semaphore_signal(barrier, inc=1, device_id=z_dev(d)[1], device_id_type=MESH)
 
     lp[:, 0:128] = jnp.zeros((8, 128), jnp.float32)
+    load_lat.wait()
     lp[:, 128:4736] = lat[...].astype(jnp.float32)
     lp[:, 4736:5248] = jnp.zeros((8, 512), jnp.float32)
     lane8 = lax.broadcasted_iota(jnp.int32, (8, 128), 1)
@@ -66,18 +76,31 @@
     lax.fori_loop(0, 4, pack, 0)
     pl.semaphore_wait(barrier, NY + NZ - 2)
 
-    first = []
-    for d in Y_ORDER:
-        other, dev = y_dev(d)
-        copy = pltpu.make_async_remote_copy(send.at[other], rx1.at[y], sa.at[d], ra.at[d], device_id=dev, device_id_type=MESH)
+    first = [None] * NY
+    for slot in range(1, NY):
+        other, dev = y_dev(SLOTS[slot])
+        copy = pltpu.make_async_remote_copy(send.at[other], rx1.at[slot], sy.at[slot], ry.at[slot], device_id=dev, device_id_type=MESH)
         copy.start()
-        first.append(copy)
-    own1 = pltpu.make_async_copy(send.at[y], rx1.at[y], loc_sem.at[0])
-    own1.start()
+        first[slot] = copy
+
+    second = []
+    for group, (lo, hi) in enumerate(GROUPS):
+        for slot in range(max(lo, 1), hi):
+            first[slot].wait_recv()
+        for d in Z_ORDER:
+            other, dev = z_dev(d)
+            source = rx1.at[lo:hi, other] if group else send.at[pl.ds(y, 1), other]
+            copy = pltpu.make_async_remote_copy(source, rx2.at[z, lo:hi], sz.at[group, d], rz.at[group, d], device_id=dev, device_id_type=MESH)
+            copy.start()
+            second.append(copy)
+    rx2[z, 0] = send[y, z]
+    rx2[z, 1:8] = rx1[1:8, z]
 
     row = lax.broadcasted_iota(jnp.int32, (256, 256), 0)
     col = lax.broadcasted_iota(jnp.int32, (256, 256), 1)
-    source = ((row >> 3) & 7) * 2 + ((row >> 6) & 1)
+    slot = (row >> 3) & 7
+    back = jnp.where((slot & 1) == 1, (slot + 1) >> 1, 8 - (slot >> 1))
+    source = ((y + 8 - back) & 7) * 2 + ((row >> 6) & 1)
     token = jnp.where(row < 128, source, 31 - source)
     target = ((row >> 2) & 1) * 128 + ((row >> 1) & 1) * 64 + token * 2 + (row & 1)
     perm[...] = jnp.where(col == target, 1.0, 0.0).astype(jnp.bfloat16)
@@ -94,21 +117,10 @@
 
     lax.fori_loop(0, 36, silu, 0)
 
-    own1.wait()
-    for copy in first:
-        copy.wait()
-
-    second = []
-    for d in Z_ORDER:
-        other, dev = z_dev(d)
-        copy = pltpu.make_async_remote_copy(rx1.at[:, other], rx2.at[z], sz.at[d], rz.at[d], device_id=dev, device_id_type=MESH)
-        copy.start()
-        second.append(copy)
-    own2 = pltpu.make_async_copy(rx1.at[:, z], rx2.at[z], loc_sem.at[1])
-    own2.start()
-    own2.wait()
     for copy in second:
         copy.wait()
+    for slot in range(1, NY):
+        first[slot].wait_send()
 
     for r in range(8):
         low = rx2[r].astype(jnp.float32).reshape(64, 128)
@@ -163,81 +175,153 @@
         lanes = slice(128 * c, 128 * c + 128)
         total = jnp.dot(cols[144:576, :], act[0:1152, lanes], preferred_element_type=jnp.float32)
         total = total + jnp.dot(cols[0:432, :], act[1152:2304, lanes], preferred_element_type=jnp.float32)
-        sb[27 * c:27 * c + 27] = total.reshape(27, 16, 128).astype(jnp.bfloat16)
-    sb[81:88] = jnp.zeros((7, 16, 128), jnp.bfloat16)
-
-    third = []
-    for d in Y_ORDER:
-        other, dev = y_dev(d)
-        copy = pltpu.make_async_remote_copy(sb.at[pl.ds(other * OWN, OWN)], rb.at[d], sc.at[d], rc.at[d], device_id=dev, device_id_type=MESH)
+        total = total.reshape(54, 8, 128).astype(jnp.bfloat16)
+        cut = min(max(USED_A - 54 * c, 0), 54)
+        if cut > 0:
+            sa[54 * c:54 * c + cut] = total[0:cut]
+        if cut < 54:
+            at = 54 * c + cut - USED_A
+            sb[at:at + 54 - cut] = total[cut:54]
+    sa[USED_A:ALL_A] = jnp.zeros((ALL_A - USED_A, 8, 128), jnp.bfloat16)
+
+    def y_copy(source, target, ssem, rsem, d):
+        return pltpu.make_async_remote_copy(source, target, ssem.at[d], rsem.at[d], device_id=y_dev(d)[1], device_id_type=MESH)
+
+    def z_copy(source, target, ssem, rsem, d):
+        return pltpu.make_async_remote_copy(source, target, ssem.at[d], rsem.at[d], device_id=z_dev(d)[1], device_id_type=MESH)
+
+    first_a = {d: y_copy(sa.at[pl.ds(y_dev(d)[0] * OWN_A, OWN_A)], ra.at[d], s1a, r1a, d) for d in Y_ORDER}
+    first_b = {d: z_copy(sb.at[pl.ds(z_dev(d)[0] * OWN_B, OWN_B)], rb.at[d], s1b, r1b, d) for d in Z_ORDER}
+    for copy in [*first_a.values(), *first_b.values()]:
         copy.start()
-        third.append(copy)
-
-    for t in range(2):
-        def backward(step, carry):
+
+    load_weight.wait()
+
+    def backward(t):
+        def one(step, carry):
             lanes = pl.ds(pl.multiple_of(step * 384, 128), 384)
             at = pl.ds(pl.multiple_of(t * 1152 + step * 384, 128), 384)
             pre = lax.dot_general(cols[(1 - t) * 144:(1 - t) * 144 + 432, lanes], weight[...], (((0,), (0,)), ((), ())), preferred_element_type=jnp.float32)
             gout[at, :] = (pre * dsl[at, :]).astype(jnp.bfloat16)
             return carry
 
-        lax.fori_loop(0, 3, backward, 0)
-    store = pltpu.make_async_copy(gout, grad_out, out_sem)
-    store.start()
-
-    for copy in third:
-        copy.wait()
-    part = sb[pl.ds(y * OWN, OWN)].astype(jnp.float32)
+        lax.fori_loop(0, 3, one, 0)
+        at = pl.ds(t * 1152, 1152)
+        store = pltpu.make_async_copy(gout.at[at], grad_out.at[at], out_sem.at[t])
+        store.start()
+        return store
+
+    stores = [backward(0)]
+
+    for copy in first_a.values():
+        copy.wait_recv()
+    part = sa[pl.ds(y * OWN_A, OWN_A)].astype(jnp.float32)
     for d in range(1, NY):
+        part = part + ra[d].astype(jnp.float32)
+    pa[...] = part
+    for d in Z_ORDER:
+        @pl.when(z_dev(d)[0] < OWN_A)
+        def _():
+            z_copy(pa.at[z_dev(d)[0]], qa.at[d], s2a, r2a, d).start()
+
+    for copy in first_b.values():
+        copy.wait_recv()
+    part = sb[pl.ds(z * OWN_B, OWN_B)].astype(jnp.float32)
+    for d in range(1, NZ):
         part = part + rb[d].astype(jnp.float32)
-    sb2[...] = part.astype(jnp.bfloat16)
-
-    for d in Z_ORDER:
-        other, dev = z_dev(d)
-
-        @pl.when(other < OWN)
-        def _():
-            pltpu.make_async_remote_copy(sb2.at[other], rb2.at[d], sd.at[d], rd.at[d], device_id=dev, device_id_type=MESH).start()
-
-    @pl.when(z < OWN)
+    pb[...] = part
+    for d in Y_ORDER:
+        @pl.when(y_dev(d)[0] < OWN_B)
+        def _():
+            y_copy(pb.at[y_dev(d)[0]], qb.at[d], s2b, r2b, d).start()
+
+    mine_a = y * OWN_A + z
+    mine_b = ALL_A + z * OWN_B + y
+
+    @pl.when(z < OWN_A)
     def _():
         for d in range(1, NZ):
-            pltpu.make_async_remote_copy(sb2.at[0], rb2.at[d], sd.at[d], rd.at[d], device_id=z_dev(d)[1], device_id_type=MESH).wait_recv()
-        whole = sb2[z].astype(jnp.float32)
+            z_copy(pa.at[0], qa.at[d], s2a, r2a, d).wait_recv()
+        whole = pa[z]
         for d in range(1, NZ):
-            whole = whole + rb2[d].astype(jnp.float32)
-        az[z] = (whole * scale).astype(jnp.bfloat16)
+            whole = whole + qa[d]
+        fin[mine_a] = (whole * scale).astype(jnp.bfloat16)
         for d in Z_ORDER:
-            pltpu.make_async_remote_copy(az.at[z], az.at[z], se.at[d], re.at[d], device_id=z_dev(d)[1], device_id_type=MESH).start()
+            z_copy(fin.at[mine_a], fin.at[mine_a], s3a, r3a, d).start()
+
+    @pl.when(y < OWN_B)
+    def _():
+        for d in range(1, NY):
+            y_copy(pb.at[0], qb.at[d], s2b, r2b, d).wait_recv()
+        whole = pb[y]
+        for d in range(1, NY):
+            whole = whole + qb[d]
+        fin[mine_b] = (whole * scale).astype(jnp.bfloat16)
+        for d in Y_ORDER:
+            y_copy(fin.at[mine_b], fin.at[mine_b], s3b, r3b, d).start()
 
     for d in range(1, NZ):
-        @pl.when(lax.rem(z + NZ - d, NZ) < OWN)
-        def _():
-            pltpu.make_async_remote_copy(az.at[0], az.at[0], se.at[d], re.at[d], device_id=z_dev(d)[1], device_id_type=MESH).wait_recv()
-
-    last = []
-    for d in Y_ORDER:
-        other, dev = y_dev(d)
-        copy = pltpu.make_async_remote_copy(az, ay.at[y], sf.at[d], rf.at[d], device_id=dev, device_id_type=MESH)
+        owner = lax.rem(z + NZ - d, NZ)
+
+        @pl.when(owner < OWN_A)
+        def _():
+            piece = fin.at[y * OWN_A + owner]
+            z_copy(piece, piece, s3a, r3a, d).wait_recv()
+    block = fin.at[pl.ds(y * OWN_A, OWN_A)]
+    last_a = {d: y_copy(block, block, s4a, r4a, d) for d in Y_ORDER}
+    for copy in last_a.values():
         copy.start()
-        last.append(copy)
-    sum_out[pl.ds(y * OWN, OWN)] = az[...]
+
+    for d in range(1, NY):
+        owner = lax.rem(y + NY - d, NY)
+
+        @pl.when(owner < OWN_B)
+        def _():
+            piece = fin.at[ALL_A + z * OWN_B + owner]
+            y_copy(piece, piece, s3b, r3b, d).wait_recv()
+    block = fin.at[pl.ds(ALL_A + z * OWN_B, OWN_B)]
+    last_b = {d: z_copy(block, block, s4b, r4b, d) for d in Z_ORDER}
+    for copy in last_b.values():
+        copy.start()
+
+    stores.append(backward(1))
+
+    for copy in [*first_a.values(), *first_b.values()]:
+        copy.wait_send()
     for d in range(1, NZ):
-        @pl.when(lax.rem(z + d, NZ) < OWN)
-        def _():
-            pltpu.make_async_remote_copy(sb2.at[0], rb2.at[d], sd.at[d], rd.at[d], device_id=z_dev(d)[1], device_id_type=MESH).wait_send()
-
-    @pl.when(z < OWN)
+        @pl.when(z_dev(d)[0] < OWN_A)
+        def _():
+            z_copy(pa.at[0], qa.at[d], s2a, r2a, d).wait_send()
+    for d in range(1, NY):
+        @pl.when(y_dev(d)[0] < OWN_B)
+        def _():
+            y_copy(pb.at[0], qb.at[d], s2b, r2b, d).wait_send()
+
+    @pl.when(z < OWN_A)
     def _():
         for d in range(1, NZ):
-            pltpu.make_async_remote_copy(az.at[0], az.at[0], se.at[d], re.at[d], device_id=z_dev(d)[1], device_id_type=MESH).wait_send()
-
-    for copy in last:
-        copy.wait()
-    for d in range(1, NY):
-        other = lax.rem(y + NY - d, NY)
-        sum_out[pl.ds(other * OWN, OWN)] = ay[other]
-    store.wait()
+            z_copy(fin.at[mine_a], fin.at[mine_a], s3a, r3a, d).wait_send()
+
+    @pl.when(y < OWN_B)
+    def _():
+        for d in range(1, NY):
+            y_copy(fin.at[mine_b], fin.at[mine_b], s3b, r3b, d).wait_send()
+
+    for d, copy in last_a.items():
+        copy.wait_send()
+        landed = fin.at[pl.ds(lax.rem(y + NY - d, NY) * OWN_A, OWN_A)]
+        y_copy(landed, landed, s4a, r4a, d).wait_recv()
+    for d, copy in last_b.items():
+        copy.wait_send()
+        landed = fin.at[pl.ds(ALL_A + lax.rem(z + NZ - d, NZ) * OWN_B, OWN_B)]
+        z_copy(landed, landed, s4b, r4b, d).wait_recv()
+    b0 = 108 - USED_A
+    sum_out[:, 0:128] = fin[0:54].astype(jnp.float32).reshape(432, 128)
+    sum_out[0:432 - 8 * b0, 128:256] = fin[54:USED_A].astype(jnp.float32).reshape(432 - 8 * b0, 128)
+    sum_out[432 - 8 * b0:432, 128:256] = fin[ALL_A:ALL_A + b0].astype(jnp.float32).reshape(8 * b0, 128)
+    sum_out[:, 256:384] = fin[ALL_A + b0:ALL_A + b0 + 54].astype(jnp.float32).reshape(432, 128)
+    for store in stores:
+        store.wait()
 
 
 def shards(latent_grad, features, head_weight):
@@ -252,11 +336,13 @@
         lambda *refs: kernel(scale, *refs),
         out_shape=(
             jax.ShapeDtypeStruct((cells, channels), bf),
-            jax.ShapeDtypeStruct((NY * OWN, 16, 128), bf),
+            jax.ShapeDtypeStruct((432, 384), f32),
         ),
-        in_specs=[vmem, hbm, vmem],
+        in_specs=[hbm, hbm, hbm],
         out_specs=(hbm, vmem),
         scratch_shapes=[
+            pltpu.VMEM((8, 4608), bf),
+            pltpu.VMEM((432, 384), bf),
             pltpu.VMEM((cells, channels), bf),
             pltpu.VMEM((cells, channels), bf),
             pltpu.VMEM((cells, channels), f32),
@@ -270,22 +356,26 @@
             pltpu.VMEM((2, 512, 128), f32),
             pltpu.VMEM((15, 64, 128), f32),
             pltpu.VMEM((576, 1152), bf),
-            pltpu.VMEM((NY * OWN, 16, 128), bf),
-            pltpu.VMEM((NY, OWN, 16, 128), bf),
-            pltpu.VMEM((OWN, 16, 128), bf),
-            pltpu.VMEM((NZ, 16, 128), bf),
-            pltpu.VMEM((OWN, 16, 128), bf),
-            pltpu.VMEM((NY, OWN, 16, 128), bf),
-            dma, dma, dma((2,)),
-            dma((NY,)), dma((NY,)), dma((NZ,)), dma((NZ,)),
+            pltpu.VMEM((ALL_A, 8, 128), bf),
+            pltpu.VMEM((NZ * OWN_B, 8, 128), bf),
+            pltpu.VMEM((NY, OWN_A, 8, 128), bf),
+            pltpu.VMEM((NZ, OWN_B, 8, 128), bf),
+            pltpu.VMEM((OWN_A, 8, 128), f32),
+            pltpu.VMEM((NZ, 8, 128), f32),
+            pltpu.VMEM((OWN_B, 8, 128), f32),
+            pltpu.VMEM((NY, 8, 128), f32),
+            pltpu.VMEM((ALL_A + NZ * OWN_B, 8, 128), bf),
+            dma((3,)), dma((2,)),
+            dma((NY,)), dma((NY,)), dma((len(GROUPS), NZ)), dma((len(GROUPS), NZ)),
             dma((NY,)), dma((NY,)), dma((NZ,)), dma((NZ,)),
             dma((NZ,)), dma((NZ,)), dma((NY,)), dma((NY,)),
+            dma((NZ,)), dma((NZ,)), dma((NY,)), dma((NY,)),
+            dma((NY,)), dma((NY,)), dma((NZ,)), dma((NZ,)),
         ],
         compiler_params=pltpu.CompilerParams(collective_id=0, has_side_effects=True),
         name="encoder_head_backward",
     )(latent_grad.T, features.reshape(cells, channels), head_weight)
-    total = total[:81].reshape(3, 432, 128).transpose(1, 0, 2).reshape(432, 384)
-    return grad.reshape(features.shape), total.astype(f32)
+    return grad.reshape(features.shape), total
 
 
 def solution(mesh):

time: 84.7 us -> 78.5 us (0.927)
  Pallas kernels: 80.1 us -> 73.1 us
    pallas_call x1, Pallas kernels: 80.1 us -> 73.1 us  [shards(): pl.pallas_call(lambda *refs: kernel(scale, *refs), out_shape=(jax.ShapeDt...]
    unnamed x4, local copies, waits for them, and re-layouts: 2.35 us -> 3.77 us
    slice x1 -> x0, local copies, waits for them, and re-layouts: 1 us -> none  [shards(): total = total[:81].reshape(3, 432, 128).transpose(1, 0, 2).reshape(432, 384)]
where the time goes in v2:
time: 78.5 us; the launch traced here: 77.5 us
  Pallas kernels  73.1 us (93%)
  local copies, waits for them, and re-layouts  3.77 us (5%)
    pallas_call x1, Pallas kernels, shards(): pl.pallas_call(lambda *refs: kernel(scale, *refs), out_shape=(jax.ShapeDt...  73.1 us
    unnamed x4, local copies, waits for them, and re-layouts  3.77 us

profile of v2, /device:TPU:6, one launch (start us, length us, event | category | flops | bytes accessed | tf_op | source)
XLA Modules:
  0.0 77.5 jit_solution(15242976620717133666)
XLA Ops:
  0.6 73.1 %encoder_head_backward.1 = (bf16[2304,384]{1,0:T(8,128)(2,1)}, f32[432,384]{1,0:T(8,128)}) custom-call(bf16[8,4608]{1,0:T(8,128)(2,1)} %bitcast.5, bf16[2304,384]{1,0:T(8,128)(2,1)} %bitcast.4, bf16[432,384]{1,0:T(8,128)(2,1)} %refs_2_.1), custom_call_target="tpu_custom_call" | custom-call | tf_op jit(solution)/shard_map/encoder_head_backward/pallas_call | solution.py:335
  73.8 0.0 copy-start
  73.8 2.9 %copy.7 = bf16[2,12,96,384]{3,2,1,0:T(8,128)(2,1)} copy(bf16[2,12,96,384]{3,2,1,0:T(8,128)(2,1)} %bitcast.3) | data formatting | bytes 3538944
  76.7 0.0 copy-done
  76.7 0.8 %copy.8 = f32[432,384]{1,0:T(8,128)} copy(f32[432,384]{1,0:T(8,128)S(1)} %copy-done) | data formatting | bytes 1327104
Async XLA Ops:
  73.8 2.9 %copy-start = (f32[432,384]{1,0:T(8,128)S(1)}, f32[432,384]{1,0:T(8,128)}, u32[]{:S(2)}) copy-start(f32[432,384]{1,0:T(8,128)} %get-tuple-element.9) | copy-start | bytes 1990660

commit v3 on v2

--- a/solution.py
+++ b/solution.py
@@ -16,11 +16,12 @@
 MESH = pl.DeviceIdType.MESH
 Y_ORDER = (4, 3, 5, 2, 6, 1, 7)
 SLOTS = (0, 1, 7, 2, 6, 3, 5, 4)
+Z_LOWER = (7, 6, 8, 5, 9, 4, 10, 3, 11, 2, 12, 1, 13, 0, 14)
 GROUPS = ((0, 1), (1, 3), (3, 5), (5, 8))
 Z_ORDER = (8, 7, 9, 6, 10, 5, 11, 4, 12, 3, 13, 2, 14, 1, 15)
 
 
-def kernel(scale, lat_hbm, feat, weight_hbm, grad_out, sum_out, lat, weight, xf, act, dsl, gout, lp, send, rx1, rx2, perm, ts, os_, gt, cols, sa, sb, ra, rb, pa, qa, pb, qb, fin, in_sem, out_sem, sy, ry, sz, rz, s1a, r1a, s1b, r1b, s2a, r2a, s2b, r2b, s3a, r3a, s3b, r3b, s4a, r4a, s4b, r4b):
+def kernel(scale, lat_hbm, feat, weight_hbm, grad_out, sum_out, weight, xf, act, dsl, lp, pk, rx1, rx2, perm, ts, os_, gt, cols, sa, sb, ra, rb, pa, qa, pb, qb, fin, in_sem, ready, sy, ry, sz, rz, s1a, r1a, s1b, r1b, s2a, r2a, s2b, r2b, s3a, r3a, s3b, r3b, s4a, r4a, s4b, r4b):
     tm = lax.axis_index("tm")
     rows = lax.axis_index("rows")
     y = lax.div(tm, 2)
@@ -35,8 +36,15 @@
         other = lax.rem(z + d, NZ)
         return other, {"tm": y * 2 + lax.div(other, 8), "rows": lax.rem(other, 8)}
 
-    load_lat = pltpu.make_async_copy(lat_hbm, lat, in_sem.at[0])
-    load_lat.start()
+    def z_at(other):
+        return {"tm": y * 2 + other // 8, "rows": other % 8}
+
+    def window(other):
+        first_tile = jnp.minimum(lax.div(9 * other, 2), 28)
+        return lat_hbm.at[:, pl.ds(pl.multiple_of(first_tile * 128, 128), 1024)]
+
+    own = pltpu.make_async_copy(window(y), rx1.at[0, :, 0:1024], in_sem.at[0])
+    own.start()
     load = pltpu.make_async_copy(feat, xf, in_sem.at[1])
     load.start()
     load_weight = pltpu.make_async_copy(weight_hbm, weight, in_sem.at[2])
@@ -45,56 +53,68 @@
     barrier = pltpu.get_barrier_semaphore()
     for d in range(1, NY):
         pl.semaphore_signal(barrier, inc=1, device_id=y_dev(d)[1], device_id_type=MESH)
-    for d in range(1, NZ):
-        pl.semaphore_signal(barrier, inc=1, device_id=z_dev(d)[1], device_id_type=MESH)
-
+    for other in range(1, NZ):
+        @pl.when(other > z)
+        def _():
+            pl.semaphore_signal(barrier, inc=1, device_id=z_at(other), device_id_type=MESH)
+    rx1[:, :, 1024:1408] = jnp.zeros((NY, 8, 384), jnp.bfloat16)
     lp[:, 0:128] = jnp.zeros((8, 128), jnp.float32)
-    load_lat.wait()
-    lp[:, 128:4736] = lat[...].astype(jnp.float32)
-    lp[:, 4736:5248] = jnp.zeros((8, 512), jnp.float32)
-    lane8 = lax.broadcasted_iota(jnp.int32, (8, 128), 1)
-
-    def pack(pair, carry):
-        base = pl.multiple_of(pair * 1152, 128)
-        for y2 in range(2):
-            for zd in range(16):
-                value = jnp.zeros((8, 128), jnp.float32)
-                for tt in range(4):
-                    start = 128 + 576 * y2 + 288 * (zd // 8) + 144 * tt + 18 * (zd % 8) - 6
-                    v, l = start // 128, start % 128
-                    shift = (32 * tt - l) % 128
-                    piece = lp[:, pl.ds(base + 128 * v, 128)]
-                    piece = pltpu.roll(piece, shift, 1) if shift else piece
-                    if l > 96:
-                        nxt = lp[:, pl.ds(base + 128 * v + 128, 128)]
-                        nxt = pltpu.roll(nxt, shift, 1) if shift else nxt
-                        piece = jnp.where(lane8 < 32 * tt + 128 - l, piece, nxt)
-                    value = piece if tt == 0 else jnp.where(lane8 < 32 * tt, value, piece)
-                send[pair * 2 + y2, zd] = value.astype(jnp.bfloat16)
-        return carry
-
-    lax.fori_loop(0, 4, pack, 0)
-    pl.semaphore_wait(barrier, NY + NZ - 2)
+    pl.semaphore_wait(barrier, NY - 1 + z)
 
     first = [None] * NY
     for slot in range(1, NY):
         other, dev = y_dev(SLOTS[slot])
-        copy = pltpu.make_async_remote_copy(send.at[other], rx1.at[slot], sy.at[slot], ry.at[slot], device_id=dev, device_id_type=MESH)
+        copy = pltpu.make_async_remote_copy(window(other), rx1.at[slot, :, 0:1024], sy.at[slot], ry.at[slot], device_id=dev, device_id_type=MESH)
         copy.start()
         first[slot] = copy
-
-    second = []
-    for group, (lo, hi) in enumerate(GROUPS):
-        for slot in range(max(lo, 1), hi):
-            first[slot].wait_recv()
-        for d in Z_ORDER:
-            other, dev = z_dev(d)
-            source = rx1.at[lo:hi, other] if group else send.at[pl.ds(y, 1), other]
-            copy = pltpu.make_async_remote_copy(source, rx2.at[z, lo:hi], sz.at[group, d], rz.at[group, d], device_id=dev, device_id_type=MESH)
-            copy.start()
-            second.append(copy)
-    rx2[z, 0] = send[y, z]
-    rx2[z, 1:8] = rx1[1:8, z]
+    for other in range(NZ - 1):
+        @pl.when(other < z)
+        def _():
+            pl.semaphore_signal(ready.at[z], inc=1, device_id=z_at(other), device_id_type=MESH)
+
+    lane8 = lax.broadcasted_iota(jnp.int32, (8, 128), 1)
+    base = pl.multiple_of(jnp.where(y == NY - 1, 384, 0), 128)
+    odd = lax.rem(y, 2) == 1
+
+    def pack(slot, carry):
+        tiles = [rx1[slot, :, pl.ds(base + 128 * j, 128)].astype(jnp.float32) for j in range(8)]
+        turned = [pltpu.roll(tile, 64, 1) for tile in tiles]
+        for j in range(7):
+            lp[:, 128 * j + 128:128 * j + 256] = jnp.where(odd, jnp.where(lane8 < 64, turned[j], turned[j + 1]), tiles[j])
+        for zd in range(NZ):
+            value = None
+            for tt in range(4):
+                start = 128 + 288 * (zd // 8) + 144 * tt + 18 * (zd % 8) - 6
+                v, l = start // 128, start % 128
+                shift = (32 * tt - l) % 128
+                piece = lp[:, 128 * v:128 * v + 128]
+                piece = pltpu.roll(piece, shift, 1) if shift else piece
+                if l > 96:
+                    nxt = lp[:, 128 * v + 128:128 * v + 256]
+                    nxt = pltpu.roll(nxt, shift, 1) if shift else nxt
+                    piece = jnp.where(lane8 < 32 * tt + 128 - l, piece, nxt)
+                value = piece if tt == 0 else jnp.where(lane8 < 32 * tt, value, piece)
+            pk[slot, zd] = value.astype(jnp.bfloat16)
+        return carry
+
+    def part_copy(group, other, source):
+        lo, hi = GROUPS[group]
+        return pltpu.make_async_remote_copy(pk.at[lo:hi, other], rx2.at[source, lo:hi], sz.at[group, other], rz.at[group, source], device_id=z_at(other), device_id_type=MESH)
+
+    def whole_copy(other, source):
+        return pltpu.make_async_remote_copy(pk.at[:, other], rx2.at[source], sz.at[0, other], rz.at[0, source], device_id=z_at(other), device_id_type=MESH)
+
+    def forward(group):
+        lo, hi = GROUPS[group]
+        for slot in range(lo, hi):
+            (own.wait if slot == 0 else first[slot].wait_recv)()
+        lax.fori_loop(lo, hi, pack, 0)
+        for other in Z_LOWER:
+            @pl.when(other < z)
+            def _():
+                part_copy(group, other, z).start()
+
+    forward(0)
 
     row = lax.broadcasted_iota(jnp.int32, (256, 256), 0)
     col = lax.broadcasted_iota(jnp.int32, (256, 256), 1)
@@ -115,10 +135,30 @@
         dsl[at, :] = sig * (1.0 + x * (1.0 - sig))
         return carry
 
-    lax.fori_loop(0, 36, silu, 0)
-
-    for copy in second:
-        copy.wait()
+    lax.fori_loop(0, 18, silu, 0)
+    forward(1)
+    lax.fori_loop(18, 36, silu, 0)
+    forward(2)
+    forward(3)
+    for other in range(1, NZ):
+        @pl.when(other > z)
+        def _():
+            pl.semaphore_wait(ready.at[other], 1)
+            whole_copy(other, z).start()
+    rx2[z] = pk[:, z]
+
+    for other in range(NZ):
+        @pl.when(other < z)
+        def _():
+            whole_copy(other, other).wait_recv()
+            for group in range(len(GROUPS)):
+                part_copy(group, other, other).wait_send()
+
+        @pl.when(other > z)
+        def _():
+            for group in range(len(GROUPS)):
+                part_copy(group, other, other).wait_recv()
+            whole_copy(other, other).wait_send()
     for slot in range(1, NY):
         first[slot].wait_send()
 
@@ -202,16 +242,12 @@
             lanes = pl.ds(pl.multiple_of(step * 384, 128), 384)
             at = pl.ds(pl.multiple_of(t * 1152 + step * 384, 128), 384)
             pre = lax.dot_general(cols[(1 - t) * 144:(1 - t) * 144 + 432, lanes], weight[...], (((0,), (0,)), ((), ())), preferred_element_type=jnp.float32)
-            gout[at, :] = (pre * dsl[at, :]).astype(jnp.bfloat16)
+            grad_out[at, :] = (pre * dsl[at, :]).astype(jnp.bfloat16)
             return carry
 
         lax.fori_loop(0, 3, one, 0)
-        at = pl.ds(t * 1152, 1152)
-        store = pltpu.make_async_copy(gout.at[at], grad_out.at[at], out_sem.at[t])
-        store.start()
-        return store
-
-    stores = [backward(0)]
+
+    backward(0)
 
     for copy in first_a.values():
         copy.wait_recv()
@@ -284,7 +320,7 @@
     for copy in last_b.values():
         copy.start()
 
-    stores.append(backward(1))
+    backward(1)
 
     for copy in [*first_a.values(), *first_b.values()]:
         copy.wait_send()
@@ -320,8 +356,6 @@
     sum_out[0:432 - 8 * b0, 128:256] = fin[54:USED_A].astype(jnp.float32).reshape(432 - 8 * b0, 128)
     sum_out[432 - 8 * b0:432, 128:256] = fin[ALL_A:ALL_A + b0].astype(jnp.float32).reshape(8 * b0, 128)
     sum_out[:, 256:384] = fin[ALL_A + b0:ALL_A + b0 + 54].astype(jnp.float32).reshape(432, 128)
-    for store in stores:
-        store.wait()
 
 
 def shards(latent_grad, features, head_weight):
@@ -335,21 +369,19 @@
     grad, total = pl.pallas_call(
         lambda *refs: kernel(scale, *refs),
         out_shape=(
-            jax.ShapeDtypeStruct((cells, channels), bf),
-            jax.ShapeDtypeStruct((432, 384), f32),
+            pltpu.VMEM((cells, channels), bf),
+            pltpu.VMEM((432, 384), f32),
         ),
         in_specs=[hbm, hbm, hbm],
-        out_specs=(hbm, vmem),
+        out_specs=(vmem, vmem),
         scratch_shapes=[
-            pltpu.VMEM((8, 4608), bf),
             pltpu.VMEM((432, 384), bf),
             pltpu.VMEM((cells, channels), bf),
             pltpu.VMEM((cells, channels), bf),
             pltpu.VMEM((cells, channels), f32),
-            pltpu.VMEM((cells, channels), bf),
-            pltpu.VMEM((8, 5248), f32),
+            pltpu.VMEM((8, 1024), f32),
             pltpu.VMEM((NY, NZ, 8, 128), bf),
-            pltpu.VMEM((NY, NZ, 8, 128), bf),
+            pltpu.VMEM((NY, 8, 1408), bf),
             pltpu.VMEM((NZ, NY, 8, 128), bf),
             pltpu.VMEM((256, 256), bf),
             pltpu.VMEM((8, 128, 128), f32),
@@ -365,7 +397,7 @@
             pltpu.VMEM((OWN_B, 8, 128), f32),
             pltpu.VMEM((NY, 8, 128), f32),
             pltpu.VMEM((ALL_A + NZ * OWN_B, 8, 128), bf),
-            dma((3,)), dma((2,)),
+            dma((3,)), pltpu.SemaphoreType.REGULAR((NZ,)),
             dma((NY,)), dma((NY,)), dma((len(GROUPS), NZ)), dma((len(GROUPS), NZ)),
             dma((NY,)), dma((NY,)), dma((NZ,)), dma((NZ,)),
             dma((NZ,)), dma((NZ,)), dma((NY,)), dma((NY,)),

time: 78.5 us -> 74.4 us (0.948)
  local copies, waits for them, and re-layouts: 3.77 us -> 2.05 us
  Pallas kernels: 73.1 us -> 71.4 us
    pallas_call x1, Pallas kernels: 73.1 us -> 71.4 us  [shards(): pl.pallas_call(lambda *refs: kernel(scale, *refs), out_shape=(pltpu.VMEM(...]
    unnamed x4 -> x2, local copies, waits for them, and re-layouts: 3.77 us -> 2.05 us
where the time goes in v3:
time: 74.4 us; the launch traced here: 74.1 us
  Pallas kernels  71.4 us (96%)
  local copies, waits for them, and re-layouts  2.05 us (3%)
    pallas_call x1, Pallas kernels, shards(): pl.pallas_call(lambda *refs: kernel(scale, *refs), out_shape=(pltpu.VMEM(...  71.4 us
    unnamed x2, local copies, waits for them, and re-layouts  2.05 us

profile of v3, /device:TPU:6, one launch (start us, length us, event | category | flops | bytes accessed | tf_op | source)
XLA Modules:
  0.0 74.1 jit_solution(361306725548700969)
XLA Ops:
  0.6 71.4 %encoder_head_backward.1 = (bf16[2304,384]{1,0:T(8,128)(2,1)S(1)}, f32[432,384]{1,0:T(8,128)S(1)}) custom-call(bf16[8,4608]{1,0:T(8,128)(2,1)} %bitcast.5, bf16[2304,384]{1,0:T(8,128)(2,1)} %bitcast.4, bf16[432,384]{1,0:T(8,128)(2,1)} %refs_2_.1), custom_call_target="tpu_custom_call" | custom-call | tf_op jit(solution)/shard_map/encoder_head_backward/pallas_call | solution.py:369
  72.0 1.2 %copy.7 = bf16[2,12,96,384]{3,2,1,0:T(8,128)(2,1)} copy(bf16[2,12,96,384]{3,2,1,0:T(8,128)(2,1)S(1)} %bitcast.3) | data formatting | bytes 3538944
  73.2 0.8 %copy.8 = f32[432,384]{1,0:T(8,128)} copy(f32[432,384]{1,0:T(8,128)S(1)} %get-tuple-element.7) | data formatting | bytes 1327104

commit v4 on v3

--- a/solution.py
+++ b/solution.py
@@ -17,7 +17,7 @@
 Y_ORDER = (4, 3, 5, 2, 6, 1, 7)
 SLOTS = (0, 1, 7, 2, 6, 3, 5, 4)
 Z_LOWER = (7, 6, 8, 5, 9, 4, 10, 3, 11, 2, 12, 1, 13, 0, 14)
-GROUPS = ((0, 1), (1, 3), (3, 5), (5, 8))
+GROUPS = 2
 Z_ORDER = (8, 7, 9, 6, 10, 5, 11, 4, 12, 3, 13, 2, 14, 1, 15)
 
 
@@ -58,7 +58,7 @@
         def _():
             pl.semaphore_signal(barrier, inc=1, device_id=z_at(other), device_id_type=MESH)
     rx1[:, :, 1024:1408] = jnp.zeros((NY, 8, 384), jnp.bfloat16)
-    lp[:, 0:128] = jnp.zeros((8, 128), jnp.float32)
+    lp[:, :, 0:128] = jnp.zeros((4, 8, 128), jnp.float32)
     pl.semaphore_wait(barrier, NY - 1 + z)
 
     first = [None] * NY
@@ -76,55 +76,57 @@
     base = pl.multiple_of(jnp.where(y == NY - 1, 384, 0), 128)
     odd = lax.rem(y, 2) == 1
 
-    def pack(slot, carry):
-        tiles = [rx1[slot, :, pl.ds(base + 128 * j, 128)].astype(jnp.float32) for j in range(8)]
-        turned = [pltpu.roll(tile, 64, 1) for tile in tiles]
-        for j in range(7):
-            lp[:, 128 * j + 128:128 * j + 256] = jnp.where(odd, jnp.where(lane8 < 64, turned[j], turned[j + 1]), tiles[j])
+    def pack(group):
+        for s in range(4):
+            tiles = [rx1[4 * group + s, :, pl.ds(base + 128 * j, 128)].astype(jnp.float32) for j in range(8)]
+            turned = [pltpu.roll(tile, 64, 1) for tile in tiles]
+            for j in range(7):
+                lp[s, :, 128 * j + 128:128 * j + 256] = jnp.where(odd, jnp.where(lane8 < 64, turned[j], turned[j + 1]), tiles[j])
         for zd in range(NZ):
-            value = None
-            for tt in range(4):
-                start = 128 + 288 * (zd // 8) + 144 * tt + 18 * (zd % 8) - 6
-                v, l = start // 128, start % 128
-                shift = (32 * tt - l) % 128
-                piece = lp[:, 128 * v:128 * v + 128]
-                piece = pltpu.roll(piece, shift, 1) if shift else piece
-                if l > 96:
-                    nxt = lp[:, 128 * v + 128:128 * v + 256]
-                    nxt = pltpu.roll(nxt, shift, 1) if shift else nxt
-                    piece = jnp.where(lane8 < 32 * tt + 128 - l, piece, nxt)
-                value = piece if tt == 0 else jnp.where(lane8 < 32 * tt, value, piece)
-            pk[slot, zd] = value.astype(jnp.bfloat16)
-        return carry
+            values = [None] * 3
+            for n in range(16):
+                s, tt = n // 4, n % 4
+                start = 128 + 288 * (zd // 8) + 144 * tt + 18 * (zd % 8) - 3
+                move = 24 * n - start
+                for v in range(start // 128, (start + 23) // 128 + 1):
+                    tile = lp[s, :, 128 * v:128 * v + 128]
+                    shift = move % 128
+                    tile = pltpu.roll(tile, shift, 1) if shift else tile
+                    lo = max(24 * n, 128 * v + move)
+                    hi = min(24 * n + 24, 128 * v + 128 + move)
+                    for j in range(lo // 128, (hi - 1) // 128 + 1):
+                        at = max(lo - 128 * j, 0)
+                        values[j] = tile if at == 0 else jnp.where(lane8 < at, values[j], tile)
+            for j in range(3):
+                pk[3 * group + j, zd] = values[j].astype(jnp.bfloat16)
 
     def part_copy(group, other, source):
-        lo, hi = GROUPS[group]
+        lo, hi = 3 * group, 3 * group + 3
         return pltpu.make_async_remote_copy(pk.at[lo:hi, other], rx2.at[source, lo:hi], sz.at[group, other], rz.at[group, source], device_id=z_at(other), device_id_type=MESH)
 
     def whole_copy(other, source):
         return pltpu.make_async_remote_copy(pk.at[:, other], rx2.at[source], sz.at[0, other], rz.at[0, source], device_id=z_at(other), device_id_type=MESH)
 
     def forward(group):
-        lo, hi = GROUPS[group]
-        for slot in range(lo, hi):
+        for slot in range(4 * group, 4 * group + 4):
             (own.wait if slot == 0 else first[slot].wait_recv)()
-        lax.fori_loop(lo, hi, pack, 0)
+        pack(group)
         for other in Z_LOWER:
             @pl.when(other < z)
             def _():
                 part_copy(group, other, z).start()
-
-    forward(0)
 
     row = lax.broadcasted_iota(jnp.int32, (256, 256), 0)
     col = lax.broadcasted_iota(jnp.int32, (256, 256), 1)
     slot = (row >> 3) & 7
     back = jnp.where((slot & 1) == 1, (slot + 1) >> 1, 8 - (slot >> 1))
     source = ((y + 8 - back) & 7) * 2 + ((row >> 6) & 1)
-    token = jnp.where(row < 128, source, 31 - source)
+    token = jnp.where(row < 128, 15 - source, source + 16)
     target = ((row >> 2) & 1) * 128 + ((row >> 1) & 1) * 64 + token * 2 + (row & 1)
     perm[...] = jnp.where(col == target, 1.0, 0.0).astype(jnp.bfloat16)
 
+    forward(0)
+    forward(1)
     load.wait()
 
     def silu(step, carry):
@@ -135,11 +137,7 @@
         dsl[at, :] = sig * (1.0 + x * (1.0 - sig))
         return carry
 
-    lax.fori_loop(0, 18, silu, 0)
-    forward(1)
-    lax.fori_loop(18, 36, silu, 0)
-    forward(2)
-    forward(3)
+    lax.fori_loop(0, 36, silu, 0)
     for other in range(1, NZ):
         @pl.when(other > z)
         def _():
@@ -151,59 +149,66 @@
         @pl.when(other < z)
         def _():
             whole_copy(other, other).wait_recv()
-            for group in range(len(GROUPS)):
+            for group in range(GROUPS):
                 part_copy(group, other, other).wait_send()
 
         @pl.when(other > z)
         def _():
-            for group in range(len(GROUPS)):
+            for group in range(GROUPS):
                 part_copy(group, other, other).wait_recv()
             whole_copy(other, other).wait_send()
     for slot in range(1, NY):
         first[slot].wait_send()
 
+    def unpack(zs):
+        parts = []
+        for group in range(GROUPS):
+            t0, t1, t2 = [rx2[zs, 3 * group + j].astype(jnp.float32) for j in range(3)]
+            parts.append(t0)
+            parts.append(jnp.where(lane8 < 32, pltpu.roll(t0, 32, 1), pltpu.roll(t1, 32, 1)))
+            parts.append(jnp.where(lane8 < 64, pltpu.roll(t1, 64, 1), pltpu.roll(t2, 64, 1)))
+            parts.append(pltpu.roll(t2, 96, 1))
+        return parts
+
     for r in range(8):
-        low = rx2[r].astype(jnp.float32).reshape(64, 128)
-        high = rx2[8 + r].astype(jnp.float32).reshape(64, 128)
-        ts[r] = jnp.concatenate([low, high], axis=0).T
+        ts[r] = jnp.concatenate(unpack(r) + unpack(8 + r), axis=0).T
     for r in range(8):
-        even = ts[r, pl.ds(0, 64, stride=2), :]
-        odd = ts[r, pl.ds(1, 64, stride=2), :]
-        left = jnp.concatenate([even, odd], axis=1).astype(jnp.bfloat16)
+        even = ts[r, pl.ds(0, 48, stride=2), :]
+        odds = ts[r, pl.ds(1, 48, stride=2), :]
+        left = jnp.concatenate([even, odds], axis=1).astype(jnp.bfloat16)
         moved = jnp.dot(left, perm[...], preferred_element_type=jnp.float32)
-        os_[0, r * 64:(r + 1) * 64, :] = moved[:, 0:128]
-        os_[1, r * 64:(r + 1) * 64, :] = moved[:, 128:256]
+        os_[0, r * 48:(r + 1) * 48, :] = moved[:, 0:128]
+        os_[1, r * 48:(r + 1) * 48, :] = moved[:, 128:256]
     top = rows == 0
     bottom = rows == 7
     for t in range(4):
-        for g in range(5):
+        for g in range(4):
             for e in range(2):
-                k0, k1, k2 = [os_[e, pl.ds(t * 16 + 3 * g + k, 8, stride=64), :] for k in range(3)]
+                k0, k1, k2 = [os_[e, pl.ds(t * 12 + 3 * g + k, 8, stride=48), :] for k in range(3)]
                 at = pl.ds(t * 16 + e, 8, stride=2)
                 k1_64 = pltpu.roll(k1, 64, 1)
                 k2_96 = pltpu.roll(k2, 96, 1)
                 k0_32 = pltpu.roll(k0, 32, 1)
-                if g > 0:
-                    v0 = jnp.where(lane8 < 64, k0, jnp.where(lane8 < 96, k1_64, k0_32))
-                    if g == 4:
-                        v0 = jnp.where(bottom, 0.0, v0)
-                    gt[3 * g, at, :] = v0
-                if 0 < g < 4:
-                    v1 = jnp.where(lane8 < 64, jnp.where(lane8 < 32, k0_32, pltpu.roll(k1, 96, 1)), jnp.where(lane8 < 96, pltpu.roll(k1, 32, 1), k2_96))
-                    gt[3 * g + 1, at, :] = v1
-                if g < 4:
-                    v2 = jnp.where(lane8 < 32, k2_96, jnp.where(lane8 < 64, k1_64, k2))
-                    if g == 0:
-                        v2 = jnp.where(top, 0.0, v2)
-                    gt[3 * g + 2, at, :] = v2
+                v0 = jnp.where(lane8 < 64, k0, jnp.where(lane8 < 96, k1_64, k0_32))
+                v1 = jnp.where(lane8 < 64, jnp.where(lane8 < 32, k0_32, pltpu.roll(k1, 96, 1)), jnp.where(lane8 < 96, pltpu.roll(k1, 32, 1), k2_96))
+                v2 = jnp.where(lane8 < 32, k2_96, jnp.where(lane8 < 64, k1_64, k2))
+                if g == 0:
+                    v0 = jnp.where(top, 0.0, v0)
+                    v1 = jnp.where(jnp.logical_and(top, lane8 < 64), 0.0, v1)
+                if g == 3:
+                    v1 = jnp.where(jnp.logical_and(bottom, lane8 >= 64), 0.0, v1)
+                    v2 = jnp.where(bottom, 0.0, v2)
+                gt[3 * g, at, :] = v0
+                gt[3 * g + 1, at, :] = v1
+                gt[3 * g + 2, at, :] = v2
 
     place = lax.rem(lax.broadcasted_iota(jnp.int32, (16, 1152), 1), 96)
     for t in range(4):
-        grid = jnp.concatenate([gt[v, 16 * t:16 * t + 16, :] for v in range(2, 13)], axis=1)
+        grid = jnp.concatenate([gt[v, 16 * t:16 * t + 16, :] for v in range(12)], axis=1)
         for kh in range(3):
             for kw in range(3):
-                off = 128 + (1 - kh) * 96 + 1 - kw
-                block = (pltpu.roll(grid, 1408 - off, 1) if off % 1408 else grid)[:, 0:1152]
+                off = 192 + (1 - kh) * 96 + 1 - kw
+                block = pltpu.roll(grid, 1536 - off, 1)[:, 0:1152]
                 if kw == 0:
                     block = jnp.where(place == 95, 0.0, block)
                 if kw == 2:
@@ -274,6 +279,17 @@
     mine_a = y * OWN_A + z
     mine_b = ALL_A + z * OWN_B + y
 
+    @pl.when(y < OWN_B)
+    def _():
+        for d in range(1, NY):
+            y_copy(pb.at[0], qb.at[d], s2b, r2b, d).wait_recv()
+        whole = pb[y]
+        for d in range(1, NY):
+            whole = whole + qb[d]
+        fin[mine_b] = (whole * scale).astype(jnp.bfloat16)
+        for d in Y_ORDER:
+            y_copy(fin.at[mine_b], fin.at[mine_b], s3b, r3b, d).start()
+
     @pl.when(z < OWN_A)
     def _():
         for d in range(1, NZ):
@@ -285,16 +301,17 @@
         for d in Z_ORDER:
             z_copy(fin.at[mine_a], fin.at[mine_a], s3a, r3a, d).start()
 
-    @pl.when(y < OWN_B)
-    def _():
-        for d in range(1, NY):
-            y_copy(pb.at[0], qb.at[d], s2b, r2b, d).wait_recv()
-        whole = pb[y]
-        for d in range(1, NY):
-            whole = whole + qb[d]
-        fin[mine_b] = (whole * scale).astype(jnp.bfloat16)
-        for d in Y_ORDER:
-            y_copy(fin.at[mine_b], fin.at[mine_b], s3b, r3b, d).start()
+    for d in range(1, NY):
+        owner = lax.rem(y + NY - d, NY)
+
+        @pl.when(owner < OWN_B)
+        def _():
+            piece = fin.at[ALL_A + z * OWN_B + owner]
+            y_copy(piece, piece, s3b, r3b, d).wait_recv()
+    block = fin.at[pl.ds(ALL_A + z * OWN_B, OWN_B)]
+    last_b = {d: z_copy(block, block, s4b, r4b, d) for d in Z_ORDER}
+    for copy in last_b.values():
+        copy.start()
 
     for d in range(1, NZ):
         owner = lax.rem(z + NZ - d, NZ)
@@ -306,18 +323,6 @@
     block = fin.at[pl.ds(y * OWN_A, OWN_A)]
     last_a = {d: y_copy(block, block, s4a, r4a, d) for d in Y_ORDER}
     for copy in last_a.values():
-        copy.start()
-
-    for d in range(1, NY):
-        owner = lax.rem(y + NY - d, NY)
-
-        @pl.when(owner < OWN_B)
-        def _():
-            piece = fin.at[ALL_A + z * OWN_B + owner]
-            y_copy(piece, piece, s3b, r3b, d).wait_recv()
-    block = fin.at[pl.ds(ALL_A + z * OWN_B, OWN_B)]
-    last_b = {d: z_copy(block, block, s4b, r4b, d) for d in Z_ORDER}
-    for copy in last_b.values():
         copy.start()
 
     backward(1)
@@ -379,14 +384,14 @@
             pltpu.VMEM((cells, channels), bf),
             pltpu.VMEM((cells, channels), bf),
             pltpu.VMEM((cells, channels), f32),
-            pltpu.VMEM((8, 1024), f32),
-            pltpu.VMEM((NY, NZ, 8, 128), bf),
+            pltpu.VMEM((4, 8, 1024), f32),
+            pltpu.VMEM((3 * GROUPS, NZ, 8, 128), bf),
             pltpu.VMEM((NY, 8, 1408), bf),
-            pltpu.VMEM((NZ, NY, 8, 128), bf),
+            pltpu.VMEM((NZ, 3 * GROUPS, 8, 128), bf),
             pltpu.VMEM((256, 256), bf),
             pltpu.VMEM((8, 128, 128), f32),
-            pltpu.VMEM((2, 512, 128), f32),
-            pltpu.VMEM((15, 64, 128), f32),
+            pltpu.VMEM((2, 384, 128), f32),
+            pltpu.VMEM((12, 64, 128), f32),
             pltpu.VMEM((576, 1152), bf),
             pltpu.VMEM((ALL_A, 8, 128), bf),
             pltpu.VMEM((NZ * OWN_B, 8, 128), bf),
@@ -398,7 +403,7 @@
             pltpu.VMEM((NY, 8, 128), f32),
             pltpu.VMEM((ALL_A + NZ * OWN_B, 8, 128), bf),
             dma((3,)), pltpu.SemaphoreType.REGULAR((NZ,)),
-            dma((NY,)), dma((NY,)), dma((len(GROUPS), NZ)), dma((len(GROUPS), NZ)),
+            dma((NY,)), dma((NY,)), dma((GROUPS, NZ)), dma((GROUPS, NZ)),
             dma((NY,)), dma((NY,)), dma((NZ,)), dma((NZ,)),
             dma((NZ,)), dma((NZ,)), dma((NY,)), dma((NY,)),
             dma((NZ,)), dma((NZ,)), dma((NY,)), dma((NY,)),

time: 74.4 us -> 71.7 us (0.964)
  Pallas kernels: 71.4 us -> 68.4 us
    pallas_call x1, Pallas kernels: 71.4 us -> 68.4 us  [shards(): pl.pallas_call(lambda *refs: kernel(scale, *refs), out_shape=(pltpu.VMEM(...]
where the time goes in v4:
time: 71.7 us; the launch traced here: 71.1 us
  Pallas kernels  68.4 us (95%)
  local copies, waits for them, and re-layouts  2.05 us (3%)
    pallas_call x1, Pallas kernels, shards(): pl.pallas_call(lambda *refs: kernel(scale, *refs), out_shape=(pltpu.VMEM(...  68.4 us
    unnamed x2, local copies, waits for them, and re-layouts  2.05 us

profile of v4, /device:TPU:6, one launch (start us, length us, event | category | flops | bytes accessed | tf_op | source)
XLA Modules:
  0.0 71.1 jit_solution(13687839402993290161)
XLA Ops:
  0.6 68.4 %encoder_head_backward.1 = (bf16[2304,384]{1,0:T(8,128)(2,1)S(1)}, f32[432,384]{1,0:T(8,128)S(1)}) custom-call(bf16[8,4608]{1,0:T(8,128)(2,1)} %bitcast.5, bf16[2304,384]{1,0:T(8,128)(2,1)} %bitcast.4, bf16[432,384]{1,0:T(8,128)(2,1)} %refs_2_.1), custom_call_target="tpu_custom_call" | custom-call | tf_op jit(solution)/shard_map/encoder_head_backward/pallas_call | solution.py:374
  69.1 1.2 %copy.7 = bf16[2,12,96,384]{3,2,1,0:T(8,128)(2,1)} copy(bf16[2,12,96,384]{3,2,1,0:T(8,128)(2,1)S(1)} %bitcast.3) | data formatting | bytes 3538944
  70.3 0.8 %copy.8 = f32[432,384]{1,0:T(8,128)} copy(f32[432,384]{1,0:T(8,128)S(1)} %get-tuple-element.7) | data formatting | bytes 1327104

commit v5 on v4

--- a/solution.py
+++ b/solution.py
@@ -9,15 +9,17 @@
 
 NY = 8
 NZ = 16
-OWN_A = 14
-OWN_B = 4
-ALL_A = 112
-USED_A = 98
+OWN_A = 15
+OWN_B = 3
+ALL_A = 120
+USED_A = 114
 MESH = pl.DeviceIdType.MESH
 Y_ORDER = (4, 3, 5, 2, 6, 1, 7)
 SLOTS = (0, 1, 7, 2, 6, 3, 5, 4)
 Z_LOWER = (7, 6, 8, 5, 9, 4, 10, 3, 11, 2, 12, 1, 13, 0, 14)
 GROUPS = 2
+Y_NEAR = (1, 7, 2, 6, 3, 5, 4)
+Z_NEAR = (1, 15, 2, 14, 3, 13, 4, 12, 5, 11, 6, 10, 7, 9, 8)
 Z_ORDER = (8, 7, 9, 6, 10, 5, 11, 4, 12, 3, 13, 2, 14, 1, 15)
 
 
@@ -216,7 +218,13 @@
                 at = (3 - t) * 144 + (kh * 3 + kw) * 16
                 cols[at:at + 16, :] = block.astype(jnp.bfloat16)
 
-    for c in range(3):
+    def y_copy(source, target, ssem, rsem, d):
+        return pltpu.make_async_remote_copy(source, target, ssem.at[d], rsem.at[d], device_id=y_dev(d)[1], device_id_type=MESH)
+
+    def z_copy(source, target, ssem, rsem, d):
+        return pltpu.make_async_remote_copy(source, target, ssem.at[d], rsem.at[d], device_id=z_dev(d)[1], device_id_type=MESH)
+
+    def weight_part(c):
         lanes = slice(128 * c, 128 * c + 128)
         total = jnp.dot(cols[144:576, :], act[0:1152, lanes], preferred_element_type=jnp.float32)
         total = total + jnp.dot(cols[0:432, :], act[1152:2304, lanes], preferred_element_type=jnp.float32)
@@ -227,17 +235,16 @@
         if cut < 54:
             at = 54 * c + cut - USED_A
             sb[at:at + 54 - cut] = total[cut:54]
+
+    weight_part(2)
+    first_b = {d: z_copy(sb.at[pl.ds(z_dev(d)[0] * OWN_B, OWN_B)], rb.at[d], s1b, r1b, d) for d in Z_ORDER}
+    for copy in first_b.values():
+        copy.start()
+    weight_part(1)
+    weight_part(0)
     sa[USED_A:ALL_A] = jnp.zeros((ALL_A - USED_A, 8, 128), jnp.bfloat16)
-
-    def y_copy(source, target, ssem, rsem, d):
-        return pltpu.make_async_remote_copy(source, target, ssem.at[d], rsem.at[d], device_id=y_dev(d)[1], device_id_type=MESH)
-
-    def z_copy(source, target, ssem, rsem, d):
-        return pltpu.make_async_remote_copy(source, target, ssem.at[d], rsem.at[d], device_id=z_dev(d)[1], device_id_type=MESH)
-
     first_a = {d: y_copy(sa.at[pl.ds(y_dev(d)[0] * OWN_A, OWN_A)], ra.at[d], s1a, r1a, d) for d in Y_ORDER}
-    first_b = {d: z_copy(sb.at[pl.ds(z_dev(d)[0] * OWN_B, OWN_B)], rb.at[d], s1b, r1b, d) for d in Z_ORDER}
-    for copy in [*first_a.values(), *first_b.values()]:
+    for copy in first_a.values():
         copy.start()
 
     load_weight.wait()
@@ -301,29 +308,41 @@
         for d in Z_ORDER:
             z_copy(fin.at[mine_a], fin.at[mine_a], s3a, r3a, d).start()
 
-    for d in range(1, NY):
+    def hand_on_b(owner):
+        piece = fin.at[ALL_A + z * OWN_B + owner]
+        for d in Z_ORDER:
+            z_copy(piece, piece, s4b, r4b, d).start()
+
+    def hand_on_a(owner):
+        piece = fin.at[y * OWN_A + owner]
+        for d in Y_ORDER:
+            y_copy(piece, piece, s4a, r4a, d).start()
+
+    @pl.when(y < OWN_B)
+    def _():
+        hand_on_b(y)
+
+    for d in Y_NEAR:
         owner = lax.rem(y + NY - d, NY)
 
         @pl.when(owner < OWN_B)
         def _():
             piece = fin.at[ALL_A + z * OWN_B + owner]
             y_copy(piece, piece, s3b, r3b, d).wait_recv()
-    block = fin.at[pl.ds(ALL_A + z * OWN_B, OWN_B)]
-    last_b = {d: z_copy(block, block, s4b, r4b, d) for d in Z_ORDER}
-    for copy in last_b.values():
-        copy.start()
-
-    for d in range(1, NZ):
+            hand_on_b(owner)
+
+    @pl.when(z < OWN_A)
+    def _():
+        hand_on_a(z)
+
+    for d in Z_NEAR:
         owner = lax.rem(z + NZ - d, NZ)
 
         @pl.when(owner < OWN_A)
         def _():
             piece = fin.at[y * OWN_A + owner]
             z_copy(piece, piece, s3a, r3a, d).wait_recv()
-    block = fin.at[pl.ds(y * OWN_A, OWN_A)]
-    last_a = {d: y_copy(block, block, s4a, r4a, d) for d in Y_ORDER}
-    for copy in last_a.values():
-        copy.start()
+            hand_on_a(owner)
 
     backward(1)
 
@@ -348,19 +367,24 @@
         for d in range(1, NY):
             y_copy(fin.at[mine_b], fin.at[mine_b], s3b, r3b, d).wait_send()
 
-    for d, copy in last_a.items():
-        copy.wait_send()
+    block = fin.at[pl.ds(y * OWN_A, OWN_A)]
+    for d in Y_NEAR:
         landed = fin.at[pl.ds(lax.rem(y + NY - d, NY) * OWN_A, OWN_A)]
+        y_copy(block, block, s4a, r4a, d).wait_send()
         y_copy(landed, landed, s4a, r4a, d).wait_recv()
-    for d, copy in last_b.items():
-        copy.wait_send()
+    block = fin.at[pl.ds(ALL_A + z * OWN_B, OWN_B)]
+    for d in Z_NEAR:
         landed = fin.at[pl.ds(ALL_A + lax.rem(z + NZ - d, NZ) * OWN_B, OWN_B)]
+        z_copy(block, block, s4b, r4b, d).wait_send()
         z_copy(landed, landed, s4b, r4b, d).wait_recv()
-    b0 = 108 - USED_A
-    sum_out[:, 0:128] = fin[0:54].astype(jnp.float32).reshape(432, 128)
-    sum_out[0:432 - 8 * b0, 128:256] = fin[54:USED_A].astype(jnp.float32).reshape(432 - 8 * b0, 128)
-    sum_out[432 - 8 * b0:432, 128:256] = fin[ALL_A:ALL_A + b0].astype(jnp.float32).reshape(8 * b0, 128)
-    sum_out[:, 256:384] = fin[ALL_A + b0:ALL_A + b0 + 54].astype(jnp.float32).reshape(432, 128)
+    for c in range(3):
+        lanes = slice(128 * c, 128 * c + 128)
+        cut = min(max(USED_A - 54 * c, 0), 54)
+        if cut > 0:
+            sum_out[0:8 * cut, lanes] = fin[54 * c:54 * c + cut].astype(jnp.float32).reshape(8 * cut, 128)
+        if cut < 54:
+            at = ALL_A + 54 * c + cut - USED_A
+            sum_out[8 * cut:432, lanes] = fin[at:at + 54 - cut].astype(jnp.float32).reshape(8 * (54 - cut), 128)
 
 
 def shards(latent_grad, features, head_weight):

time: 71.7 us -> 71.2 us (level)
  no operation moved by 1% of the time
where the time goes in v5:
time: 71.2 us; the launch traced here: 71 us
  Pallas kernels  68.3 us (96%)
  local copies, waits for them, and re-layouts  2.05 us (3%)
    pallas_call x1, Pallas kernels, shards(): pl.pallas_call(lambda *refs: kernel(scale, *refs), out_shape=(pltpu.VMEM(...  68.3 us
    unnamed x2, local copies, waits for them, and re-layouts  2.05 us

profile of v5, /device:TPU:6, one launch (start us, length us, event | category | flops | bytes accessed | tf_op | source)
XLA Modules:
  0.0 71.0 jit_solution(2633760809492358463)
XLA Ops:
  0.6 68.3 %encoder_head_backward.1 = (bf16[2304,384]{1,0:T(8,128)(2,1)S(1)}, f32[432,384]{1,0:T(8,128)S(1)}) custom-call(bf16[8,4608]{1,0:T(8,128)(2,1)} %bitcast.5, bf16[2304,384]{1,0:T(8,128)(2,1)} %bitcast.4, bf16[432,384]{1,0:T(8,128)(2,1)} %refs_2_.1), custom_call_target="tpu_custom_call" | custom-call | tf_op jit(solution)/shard_map/encoder_head_backward/pallas_call | solution.py:398
  68.9 1.2 %copy.7 = bf16[2,12,96,384]{3,2,1,0:T(8,128)(2,1)} copy(bf16[2,12,96,384]{3,2,1,0:T(8,128)(2,1)S(1)} %bitcast.3) | data formatting | bytes 3538944
  70.1 0.8 %copy.8 = f32[432,384]{1,0:T(8,128)} copy(f32[432,384]{1,0:T(8,128)S(1)} %get-tuple-element.7) | data formatting | bytes 1327104

commit v6 on v5

--- a/solution.py
+++ b/solution.py
@@ -283,6 +283,7 @@
         def _():
             y_copy(pb.at[y_dev(d)[0]], qb.at[d], s2b, r2b, d).start()
 
+    backward(1)
     mine_a = y * OWN_A + z
     mine_b = ALL_A + z * OWN_B + y
 
@@ -344,7 +345,6 @@
             z_copy(piece, piece, s3a, r3a, d).wait_recv()
             hand_on_a(owner)
 
-    backward(1)
 
     for copy in [*first_a.values(), *first_b.values()]:
         copy.wait_send()
@@ -385,6 +385,17 @@
         if cut < 54:
             at = ALL_A + 54 * c + cut - USED_A
             sum_out[8 * cut:432, lanes] = fin[at:at + 54 - cut].astype(jnp.float32).reshape(8 * (54 - cut), 128)
+
+
+def store(grad, total, grad_out, total_out, sem):
+    copies = [pltpu.make_async_copy(total, total_out, sem.at[0])]
+    for i in range(4):
+        at = pl.ds(576 * i, 576)
+        copies.append(pltpu.make_async_copy(grad.at[at], grad_out.at[at], sem.at[1 + i]))
+    for copy in copies:
+        copy.start()
+    for copy in copies:
+        copy.wait()
 
 
 def shards(latent_grad, features, head_weight):
@@ -436,6 +447,17 @@
         compiler_params=pltpu.CompilerParams(collective_id=0, has_side_effects=True),
         name="encoder_head_backward",
     )(latent_grad.T, features.reshape(cells, channels), head_weight)
+    grad, total = pl.pallas_call(
+        store,
+        out_shape=(
+            jax.ShapeDtypeStruct((cells, channels), bf),
+            jax.ShapeDtypeStruct((432, 384), f32),
+        ),
+        in_specs=[hbm, hbm],
+        out_specs=(hbm, hbm),
+        scratch_shapes=[dma((5,))],
+        name="store_results",
+    )(*[pltpu.with_memory_space_constraint(x, pltpu.VMEM) for x in (grad, total)])
     return grad.reshape(features.shape), total
 
 

time: 71.2 us -> 70.6 us (level)
  local copies, waits for them, and re-layouts: 2.05 us -> 0 us
  Pallas kernels: 68.3 us -> 69.8 us
    unnamed x2 -> x0, local copies, waits for them, and re-layouts: 2.05 us -> none
    pallas_call x0 -> x1, Pallas kernels: none -> 1.46 us  [shards(): pl.pallas_call(store, out_shape=(jax.ShapeDtypeStruct((cells, channels),...]
where the time goes in v6:
time: 70.6 us; the launch traced here: 70.4 us
  Pallas kernels  69.8 us (99%)
    pallas_call x1, Pallas kernels, shards(): pl.pallas_call(lambda *refs: kernel(scale, *refs), out_shape=(pltpu.VMEM(...  68.3 us
    pallas_call x1, Pallas kernels, shards(): pl.pallas_call(store, out_shape=(jax.ShapeDtypeStruct((cells, channels),...  1.46 us

profile of v6, /device:TPU:6, one launch (start us, length us, event | category | flops | bytes accessed | tf_op | source)
XLA Modules:
  0.0 70.4 jit_solution(355345152443947103)
XLA Ops:
  0.6 68.3 %encoder_head_backward.1 = (bf16[2304,384]{1,0:T(8,128)(2,1)S(1)}, f32[432,384]{1,0:T(8,128)S(1)}) custom-call(bf16[8,4608]{1,0:T(8,128)(2,1)} %bitcast.4, bf16[2304,384]{1,0:T(8,128)(2,1)} %bitcast.3, bf16[432,384]{1,0:T(8,128)(2,1)} %refs_2_.1), custom_call_target="tpu_custom_call" | custom-call | tf_op jit(solution)/shard_map/encoder_head_backward/pallas_call | solution.py:409
  68.9 1.5 %store_results.1 = (bf16[2304,384]{1,0:T(8,128)(2,1)}, f32[432,384]{1,0:T(8,128)}) custom-call(bf16[2304,384]{1,0:T(8,128)(2,1)S(1)} %get-tuple-element.6.grad, f32[432,384]{1,0:T(8,128)S(1)} %get-tuple-element.7.total), custom_call_target="tpu_custom_call" | custom-call | tf_op jit(solution)/shard_map/store_results/pallas_call | solution.py:450

commit v7 on v6

--- a/solution.py
+++ b/solution.py
@@ -64,7 +64,7 @@
     pl.semaphore_wait(barrier, NY - 1 + z)
 
     first = [None] * NY
-    for slot in range(1, NY):
+    for slot in reversed(range(1, NY)):
         other, dev = y_dev(SLOTS[slot])
         copy = pltpu.make_async_remote_copy(window(other), rx1.at[slot, :, 0:1024], sy.at[slot], ry.at[slot], device_id=dev, device_id_type=MESH)
         copy.start()

time: 70.6 us -> 72.5 us (1.027)
  Pallas kernels: 69.8 us -> 71.7 us
    pallas_call x1, Pallas kernels: 68.3 us -> 70.2 us  [shards(): pl.pallas_call(lambda *refs: kernel(scale, *refs), out_shape=(pltpu.VMEM(...]
where the time goes in v7:
time: 72.5 us; the launch traced here: 72.3 us
  Pallas kernels  71.7 us (99%)
    pallas_call x1, Pallas kernels, shards(): pl.pallas_call(lambda *refs: kernel(scale, *refs), out_shape=(pltpu.VMEM(...  70.2 us
    pallas_call x1, Pallas kernels, shards(): pl.pallas_call(store, out_shape=(jax.ShapeDtypeStruct((cells, channels),...  1.46 us

profile of v7, /device:TPU:6, one launch (start us, length us, event | category | flops | bytes accessed | tf_op | source)
XLA Modules:
  0.0 72.3 jit_solution(5200334073890905191)
XLA Ops:
  0.6 70.2 %encoder_head_backward.1 = (bf16[2304,384]{1,0:T(8,128)(2,1)S(1)}, f32[432,384]{1,0:T(8,128)S(1)}) custom-call(bf16[8,4608]{1,0:T(8,128)(2,1)} %bitcast.4, bf16[2304,384]{1,0:T(8,128)(2,1)} %bitcast.3, bf16[432,384]{1,0:T(8,128)(2,1)} %refs_2_.1), custom_call_target="tpu_custom_call" | custom-call | tf_op jit(solution)/shard_map/encoder_head_backward/pallas_call | solution.py:409
  70.8 1.5 %store_results.1 = (bf16[2304,384]{1,0:T(8,128)(2,1)}, f32[432,384]{1,0:T(8,128)}) custom-call(bf16[2304,384]{1,0:T(8,128)(2,1)S(1)} %get-tuple-element.6.grad, f32[432,384]{1,0:T(8,128)S(1)} %get-tuple-element.7.total), custom_call_target="tpu_custom_call" | custom-call | tf_op jit(solution)/shard_map/store_results/pallas_call | solution.py:450
